TPU v7x, 128 devices: a whole 4x4x4 slice. The times are simulated.
128 devices in a mesh: var: 16 (over x_hi, z, core), tp: 8 (over y, x_lo).
Axes of the slice: x: 4 (x_hi: 2, x_lo: 2; x = x_hi * 2 + x_lo), y: 4, z: 4, core: 2. Of those that a mesh axis runs over, the one named last changes fastest.
Arguments:
- hidden_in: bfloat16 [48, 384, 2048], P('var'), may hold values from -100 to 100
- run_table: int32 [48, 2], P('var'), may hold values 0 or 1
- qkv_weight: bfloat16 [2048, 3072], P('var', 'tp'), may hold values from -1 to 1
- out_weight: bfloat16 [2048, 2048], P('tp', 'var'), may hold values from -0.125 to 0.125
- gate_up_weight: bfloat16 [2048, 2, 8192], P('var', None, 'tp'), may hold values from -0.125 to 0.125
- down_weight: bfloat16 [8192, 2048], P('tp', 'var'), may hold values from -0.0625 to 0.0625
Outputs:
- layer_out: bfloat16 [48, 384, 2048], P('var')
All inputs are finite; a program needn't handle non-finite values. No bound on the sum of `run_table` on one device may be relied on, other than what follows from the above.
Results may differ from a plain program's by a relative error of at most 0.0075.
Values may be sent and summed in bfloat16 or wider, within the bound.
No kernel may reach another device: no remote copies, remote signals or barrier semaphores. Data moves between devices by JAX's collectives and lax.ppermute only.
A program may use at most 128 MiB of HBM per device.

v0:
```python
import functools

import jax
import jax.numpy as jnp
from jax import lax
from jax.experimental import pallas as pl
from jax.experimental.pallas import tpu as pltpu
from jax.sharding import PartitionSpec as P


QUERY_HEADS = 32
HEAD_SIZE = 64
BF = jnp.bfloat16
F32 = jnp.float32

VAR_XH = [(v, v ^ 8) for v in range(16)]
VAR_CORE = [(v, v ^ 1) for v in range(16)]
TP_XL = [(t, t ^ 1) for t in range(8)]
PAIR_FIRST = [(0, 0), (0, 1), (1, 0), (1, 1), (3, 0), (3, 1), (2, 0), (2, 1)]
RING_FIRST = [(0, 0), (1, 0), (3, 0), (2, 0), (0, 1), (1, 1), (3, 1), (2, 1)]
LANES = 128


def var_z(step):
    return [(v, (v & 9) | ((((v >> 1) & 3) + step) % 4) << 1) for v in range(16)]


def tp_y(step, pair=0):
    return [(t, (t & 1) ^ pair | (((t >> 1) + step) % 4) << 1) for t in range(8)]


VAR = ("var", VAR_XH, var_z(1), var_z(3))
TP = ("tp", TP_XL, tp_y(1), tp_y(3))


def halves(pair, axis):
    return lax.split(pair, [pair.shape[axis] // 2] * 2, axis=axis)


def gather_pair_first(piece, axis, group):
    name, flip, up, down = group
    own = jnp.concatenate([piece, lax.ppermute(piece, name, flip)], axis=axis)
    back = lax.ppermute(own, name, up)
    ahead = lax.ppermute(own, name, down)
    far = [
        lax.ppermute(halves(back, axis)[0], name, up),
        lax.ppermute(halves(ahead, axis)[1], name, down),
    ]
    return [own, back, ahead] + far


def send_both(piece, group):
    return lax.ppermute(piece, group[0], group[2]), lax.ppermute(piece, group[0], group[3])


def gather_each(piece, group):
    name, flip, up, down = group
    other = lax.ppermute(piece, name, flip)
    back = lax.ppermute(piece, name, up)
    ahead = lax.ppermute(piece, name, down)
    other_back = lax.ppermute(other, name, up)
    other_ahead = lax.ppermute(other, name, down)
    far = lax.ppermute(back, name, up)
    other_far = lax.ppermute(other_ahead, name, down)
    return [piece, other, back, other_back, ahead, other_ahead, far, other_far]


def gather_ring(piece, group):
    name, _, up, down = group
    back = lax.ppermute(piece, name, up)
    ahead = lax.ppermute(piece, name, down)
    return [piece, back, ahead, lax.ppermute(back, name, up)]


def cross_each(pieces, group):
    return [lax.ppermute(piece, group[0], group[1]) for piece in pieces]


def compiler_params(mib):
    return pltpu.CompilerParams(vmem_limit_bytes=mib * 2**20)


def dot(a, b):
    return jnp.dot(a, b, preferred_element_type=F32)


def lanes(block):
    return pl.ds(pl.multiple_of(block * LANES, LANES), LANES)


def norm_scale(widened):
    return lax.rsqrt(jnp.mean(widened * widened, axis=-1, keepdims=True) + 1e-05)


def normed_blocks_kernel(place_ref, in_ref, out_ref):
    @pl.loop(0, in_ref.shape[0] // 64)
    def _(i):
        rows = pl.ds(pl.multiple_of(i * 64, 64), 64)
        scale = norm_scale(in_ref[rows, :].astype(F32))
        for j in range(16):
            block = in_ref[rows, lanes(place_ref[j])].astype(F32)
            out_ref[rows, j * LANES : (j + 1) * LANES] = (block * scale).astype(BF)


def normed_blocks(place, tensor):
    rows, columns = tensor.shape
    step = 384
    return pl.pallas_call(
        normed_blocks_kernel,
        out_shape=jax.ShapeDtypeStruct(tensor.shape, BF),
        grid_spec=pltpu.PrefetchScalarGridSpec(
            num_scalar_prefetch=1,
            grid=(rows // step,),
            in_specs=[pl.BlockSpec((step, columns), lambda i, place_ref: (i, 0))],
            out_specs=pl.BlockSpec((step, columns), lambda i, place_ref: (i, 0)),
        ),
        compiler_params=compiler_params(58),
        cost_estimate=pl.CostEstimate(
            flops=4 * rows * columns, bytes_accessed=4 * rows * columns, transcendentals=rows
        ),
        name="normed_blocks",
    )(place, tensor)


def row_switch(run_ref, column, first_row, rows, full_len, seq_count):
    row = first_row + lax.broadcasted_iota(jnp.int32, (rows, 1), 0)
    switch = jnp.zeros((rows, 1), F32)
    for s in range(seq_count):
        inside = (row >= s * full_len) & (row < (s + 1) * full_len)
        switch = jnp.where(inside, run_ref[2 * s + column].astype(F32), switch)
    return switch


def project_kernel(counts, place_ref, own_ref, other_ref, *refs):
    weight_refs = refs[: sum(counts)]
    own_out, other_out = refs[sum(counts) :]
    rows, width = own_ref.shape[1:]
    first = 0
    for group, count in enumerate(counts):
        entry = 16 + 8 * group
        term = None
        for weight_ref in weight_refs[:count]:
            for i in range(weight_ref.shape[0] // width):
                source = place_ref[entry]
                heads = jnp.concatenate([own_ref[source], other_ref[source]], axis=0)
                product = dot(heads, weight_ref[i * width : (i + 1) * width, :])
                term = product if term is None else term + product
                entry += 1
        at = slice(first, first + term.shape[1])
        own_out[:, at] = term[:rows]
        other_out[:, at] = term[rows:].astype(BF)
        first += term.shape[1]
        weight_refs = weight_refs[count:]


def project(place, own_heads, other_heads, groups):
    count, rows, width = own_heads.shape
    weights = sum(groups, [])
    columns = sum(group[0].shape[1] for group in groups)
    whole = lambda k, *refs: (0, 0)
    heads = pl.BlockSpec((count, rows, width), lambda k, *refs: (0, 0, 0))
    return pl.pallas_call(
        functools.partial(project_kernel, [len(group) for group in groups]),
        out_shape=[jax.ShapeDtypeStruct((rows, columns), kind) for kind in (F32, BF)],
        grid_spec=pltpu.PrefetchScalarGridSpec(
            num_scalar_prefetch=1,
            grid=(1,),
            in_specs=[heads, heads] + [pl.BlockSpec(w.shape, whole) for w in weights],
            out_specs=[pl.BlockSpec((rows, columns), whole)] * 2,
        ),
        compiler_params=compiler_params(58),
        cost_estimate=pl.CostEstimate(
            flops=4 * rows * count * width * columns,
            bytes_accessed=2 * count * width * columns,
            transcendentals=0,
        ),
        name="project",
    )(place, own_heads, other_heads, *weights)


def combine_kernel(full_len, place_ref, run_ref, tp_ref, one_ref, two_ref, hidden_ref, *refs):
    after_ref, normed_a, normed_b, switch_ref = refs
    rows, _ = one_ref.shape
    first_row = tp_ref[0] * rows
    seq_count = run_ref.shape[0] // 2
    switch = row_switch(run_ref, 0, first_row, rows, full_len, seq_count)
    for j in range(16):
        at = slice(j * LANES, (j + 1) * LANES)
        source = one_ref if j < 8 else two_ref
        attention = source[:, j % 8 * LANES : (j % 8 + 1) * LANES].astype(F32)
        residual = hidden_ref[:, lanes(place_ref[j])].astype(F32)
        after_ref[:, at] = (residual + switch * attention).astype(BF)
    switch = row_switch(run_ref, 1, first_row, rows, full_len, seq_count)
    switch_ref[...] = jnp.broadcast_to(switch, switch_ref.shape)
    widened = after_ref[...].astype(F32)
    normed = (widened * norm_scale(widened)).astype(BF)
    split = normed_a.shape[0]
    normed_a[...] = normed[:split]
    normed_b[...] = normed[split:]


def combine(place, run_flat, tp_flat, one, two, flat_hidden, full_len, split):
    rows, half = one.shape
    columns = flat_hidden.shape[1]
    whole = lambda k, *refs: (0, 0)
    counts = (rows, split, rows - split)
    return pl.pallas_call(
        functools.partial(combine_kernel, full_len),
        out_shape=[jax.ShapeDtypeStruct((n, columns), BF) for n in counts]
        + [jax.ShapeDtypeStruct((rows, LANES), F32)],
        grid_spec=pltpu.PrefetchScalarGridSpec(
            num_scalar_prefetch=3,
            grid=(1,),
            in_specs=[pl.BlockSpec((rows, half), whole)] * 2
            + [pl.BlockSpec((rows, columns), lambda k, place, run, tp: (tp[0], 0))],
            out_specs=[pl.BlockSpec((n, columns), whole) for n in counts]
            + [pl.BlockSpec((rows, LANES), whole)],
        ),
        compiler_params=compiler_params(58),
        cost_estimate=pl.CostEstimate(
            flops=8 * rows * columns, bytes_accessed=12 * rows * columns, transcendentals=rows
        ),
        name="combine",
    )(place, run_flat, tp_flat, one, two, flat_hidden)


def collect_rows(in_refs, rows_ref, total):
    at = 0
    for ref in in_refs:
        rows_ref[at : at + ref.shape[0], :] = ref[...]
        at += ref.shape[0]
    total[...] = jnp.zeros_like(total)


def add_block(rows_ref, gate_ref, up_ref, down_ref, total):
    rows = rows_ref[...]
    gate = dot(rows, gate_ref[...])
    up = dot(rows, up_ref[...])
    hidden = (gate / (1.0 + jnp.exp(-gate)) * up).astype(BF)
    total[...] += dot(hidden, down_ref[...])


def store_rows(total, outs, out_refs):
    for ranges, ref in zip(outs, out_refs):
        to = 0
        for first, rows in ranges:
            ref[to : to + rows, :] = total[first : first + rows, :].astype(BF)
            to += rows


def lengths(outs):
    return [sum(rows for _, rows in ranges) for ranges in outs]


def first_feed_forward_kernel(n_weights, n_in, outs, *refs):
    gates, ups, downs = (refs[i * n_weights : (i + 1) * n_weights] for i in range(3))
    refs = refs[3 * n_weights :]
    in_refs, out_refs = refs[:n_in], refs[n_in:-5]
    gate_ref, up_ref, down_ref, rows_ref, total = refs[-5:]
    step = pl.program_id(0)
    pl.when(step == 0)(lambda: collect_rows(in_refs, rows_ref, total))
    width = gate_ref.shape[1]
    at = 0
    for gate_piece, up_piece, down_piece in zip(gates, ups, downs):
        depth = gate_piece.shape[0]
        gate_ref[at : at + depth, :] = gate_piece[...]
        up_ref[at : at + depth, :] = up_piece[...]
        for v in range(depth // LANES):
            to = at + v * LANES
            for j in range(width // LANES):
                down_ref[j * LANES : (j + 1) * LANES, to : to + LANES] = down_piece[
                    v * LANES : (v + 1) * LANES, j * LANES : (j + 1) * LANES
                ]
        at += depth
    add_block(rows_ref, gate_ref, up_ref, down_ref, total)
    pl.when(step == pl.num_programs(0) - 1)(lambda: store_rows(total, outs, out_refs))


def feed_forward_kernel(n_in, outs, gate_ref, up_ref, down_ref, *refs):
    in_refs, out_refs, rows_ref, total = refs[:n_in], refs[n_in:-2], refs[-2], refs[-1]
    step = pl.program_id(0)
    pl.when(step == 0)(lambda: collect_rows(in_refs, rows_ref, total))
    add_block(rows_ref, gate_ref, up_ref, down_ref, total)
    pl.when(step == pl.num_programs(0) - 1)(lambda: store_rows(total, outs, out_refs))


def feed_forward_cost(rows, columns, ff):
    return pl.CostEstimate(
        flops=6 * rows * columns * ff,
        bytes_accessed=6 * columns * ff + 4 * rows * columns,
        transcendentals=rows * ff,
    )


def weight_specs(columns, width):
    return [
        pl.BlockSpec((columns, width), lambda j: (0, j)),
        pl.BlockSpec((columns, width), lambda j: (0, j)),
        pl.BlockSpec((width, columns), lambda j: (j, 0)),
    ]


FF_WIDTH = 256


def first_feed_forward(pieces, outs, weights, ff):
    columns = sum(weight.shape[0] for weight in weights)
    rows = sum(piece.shape[0] for piece in pieces)
    width = FF_WIDTH
    steps = ff // width
    whole = lambda j: (0, 0)

    def specs(first):
        return [pl.BlockSpec((w.shape[0], width), lambda j: (0, j + first)) for w in weights]

    return pl.pallas_call(
        functools.partial(first_feed_forward_kernel, len(weights), len(pieces), outs),
        out_shape=[jax.ShapeDtypeStruct((n, columns), BF) for n in lengths(outs)]
        + [jax.ShapeDtypeStruct(dims, BF) for dims in [(columns, ff)] * 2 + [(ff, columns)]],
        grid=(steps,),
        in_specs=specs(0)
        + specs(steps)
        + specs(2 * steps)
        + [pl.BlockSpec(piece.shape, whole) for piece in pieces],
        out_specs=[pl.BlockSpec((n, columns), whole) for n in lengths(outs)] + weight_specs(columns, width),
        scratch_shapes=[pltpu.VMEM((rows, columns), BF), pltpu.VMEM((rows, columns), F32)],
        compiler_params=compiler_params(58),
        cost_estimate=feed_forward_cost(rows, columns, ff),
        name="first_feed_forward",
    )(*weights, *weights, *weights, *pieces)


def feed_forward(pieces, outs, weights):
    columns, ff = weights[0].shape
    rows = sum(piece.shape[0] for piece in pieces)
    whole = lambda j: (0, 0)
    return pl.pallas_call(
        functools.partial(feed_forward_kernel, len(pieces), outs),
        out_shape=[jax.ShapeDtypeStruct((n, columns), BF) for n in lengths(outs)],
        grid=(ff // FF_WIDTH,),
        in_specs=weight_specs(columns, FF_WIDTH)
        + [pl.BlockSpec(piece.shape, whole) for piece in pieces],
        out_specs=[pl.BlockSpec((n, columns), whole) for n in lengths(outs)],
        scratch_shapes=[pltpu.VMEM((rows, columns), BF), pltpu.VMEM((rows, columns), F32)],
        compiler_params=compiler_params(58),
        cost_estimate=feed_forward_cost(rows, columns, ff),
        name="feed_forward",
    )(*weights, *pieces)


def place_pieces_kernel(items, place_ref, *refs):
    in_refs, (out_ref, held, sems) = refs[: len(items)], refs[-3:]
    copies = []
    at = 0
    for i, (entry, first) in enumerate(items):
        rows = in_refs[i].shape[0]
        for j in range(16):
            block = in_refs[i][:, j * LANES : (j + 1) * LANES]
            held[at : at + rows, lanes(place_ref[j])] = block
        target = out_ref.at[place_ref[entry], pl.ds(first, rows)]
        copies.append(pltpu.make_async_copy(held.at[pl.ds(at, rows)], target, sems.at[i]))
        copies[-1].start()
        at += rows
    for copy in copies:
        copy.wait()


def place_pieces(place, pieces, items, shape, earlier=None):
    block = lambda i, place_ref: (0, 0)
    held = [] if earlier is None else [earlier]
    return pl.pallas_call(
        functools.partial(place_pieces_kernel, items),
        out_shape=jax.ShapeDtypeStruct(shape, BF),
        grid_spec=pltpu.PrefetchScalarGridSpec(
            num_scalar_prefetch=1,
            grid=(1,),
            in_specs=[pl.BlockSpec(piece.shape, block) for piece in pieces]
            + [pl.BlockSpec(memory_space=pltpu.HBM)] * len(held),
            out_specs=pl.BlockSpec(memory_space=pltpu.HBM),
            scratch_shapes=[
                pltpu.VMEM((sum(piece.shape[0] for piece in pieces), shape[2]), BF),
                pltpu.SemaphoreType.DMA((len(items),)),
            ],
        ),
        input_output_aliases={1 + len(pieces): 0} if held else {},
        compiler_params=compiler_params(58),
        cost_estimate=pl.CostEstimate(
            flops=0, bytes_accessed=4 * sum(piece.size for piece in pieces), transcendentals=0
        ),
        name="place_pieces",
    )(place, *pieces, *held)


def places(var_index, tp_index):
    table = PAIR_FIRST + PAIR_FIRST + PAIR_FIRST + RING_FIRST
    back = jnp.array([b for b, _ in table], jnp.int32)
    pair = jnp.array([p for _, p in table], jnp.int32)
    item = jnp.arange(32, dtype=jnp.int32)
    other = (item // 8) % 2
    blocks = ((var_index // 8) ^ pair) * 8 + (((var_index // 2) - back) & 3) * 2
    blocks = blocks + ((var_index % 2) ^ other)
    sources = (((tp_index // 2) - back) & 3) * 2 + ((tp_index % 2) ^ pair)
    return jnp.where(item < 16, blocks, sources).astype(jnp.int32)


def rotary_tables(full_len):
    column = jnp.arange(LANES, dtype=jnp.int32)
    half_width = HEAD_SIZE // 2
    exponent = (column % half_width).astype(F32) * (2.0 / HEAD_SIZE)
    frequency = jnp.power(F32(500000.0), -exponent)
    angles = jnp.arange(full_len, dtype=F32)[:, None] * frequency[None, :]
    sign = jnp.where(column % HEAD_SIZE < half_width, F32(-1.0), F32(1.0))[None, :]
    return jnp.cos(angles), jnp.sin(angles) * sign


def attention_kernel(rows_ref, one_ref, two_ref, cosine_ref, sine_ref, out_ref):
    half, width = one_ref.shape
    length = rows_ref.shape[0]
    projected = dot(rows_ref[:, :half], one_ref[...]) + dot(rows_ref[:, half:], two_ref[...])
    half_width = HEAD_SIZE // 2
    column = lax.broadcasted_iota(jnp.int32, (length, LANES), 1)
    lower = (column & half_width) == 0
    tiles = []
    for first in range(0, width, LANES):
        tile = projected[:, first : first + LANES]
        swapped = jnp.where(
            lower,
            pltpu.roll(tile, LANES - half_width, 1),
            pltpu.roll(tile, half_width, 1),
        )
        turned = tile * cosine_ref[...] + swapped * sine_ref[...]
        if first + LANES == width:
            turned = jnp.where(column < HEAD_SIZE, turned, tile)
        tiles.append(turned.astype(BF))
    keys = tiles[-1][:, :HEAD_SIZE]
    values = tiles[-1][:, HEAD_SIZE:]
    causal = lax.broadcasted_iota(jnp.int32, (length, length), 0) >= lax.broadcasted_iota(
        jnp.int32, (length, length), 1
    )
    for h in range(width // HEAD_SIZE - 2):
        lane = h * HEAD_SIZE % LANES
        query = tiles[h * HEAD_SIZE // LANES][:, lane : lane + HEAD_SIZE]
        scores = lax.dot_general(
            query, keys, (((1,), (1,)), ((), ())), preferred_element_type=F32
        ) * (HEAD_SIZE**-0.5)
        scores = jnp.where(causal, scores, F32(-1e30))
        exped = jnp.exp(scores - jnp.max(scores, axis=-1, keepdims=True))
        probs = (exped / jnp.sum(exped, axis=-1, keepdims=True)).astype(BF)
        out_ref[:, h * HEAD_SIZE : (h + 1) * HEAD_SIZE] = dot(probs, values).astype(BF)


def attention(rows, one, two, width, cosine, sine):
    row_count, model_width = rows.shape
    half = one.shape[0]
    full_len = cosine.shape[0]
    out_width = width - 2 * HEAD_SIZE
    whole = lambda i: (0, 0)
    return pl.pallas_call(
        attention_kernel,
        out_shape=jax.ShapeDtypeStruct((row_count, out_width), BF),
        grid=(row_count // full_len,),
        in_specs=[
            pl.BlockSpec((full_len, model_width), lambda i: (i, 0)),
            pl.BlockSpec((half, width), whole),
            pl.BlockSpec((half, width), whole),
            pl.BlockSpec(cosine.shape, whole),
            pl.BlockSpec(sine.shape, whole),
        ],
        out_specs=pl.BlockSpec((full_len, out_width), lambda i: (i, 0)),
        compiler_params=compiler_params(58),
        cost_estimate=pl.CostEstimate(
            flops=2 * row_count * width * model_width + 4 * row_count * full_len * out_width,
            bytes_accessed=2 * row_count * model_width + 4 * half * width,
            transcendentals=row_count * full_len * 4,
        ),
        name="attention",
    )(rows, one, two, cosine, sine)


def after(value, *earlier):
    return lax.optimization_barrier((value,) + earlier)[0]


def layer(hidden_in, run_table, qkv_weight, out_weight, gate_up_weight, down_weight):
    tp_count = lax.axis_size("tp")
    seq_count, full_len, model_width = hidden_in.shape
    row_count = seq_count * full_len
    own_rows = row_count // tp_count
    query_slice = QUERY_HEADS // tp_count
    tp_index = lax.axis_index("tp")
    half = model_width // 2
    place = places(lax.axis_index("var"), tp_index)
    tp_flat = tp_index.astype(jnp.int32).reshape(1)
    run_flat = run_table.reshape(-1)

    def from_partner(tensor):
        return lax.ppermute(tensor, "var", VAR_CORE)

    block = qkv_weight.shape[0]
    width = qkv_weight.shape[1]
    heads_width = query_slice * HEAD_SIZE
    ff_local = gate_up_weight.shape[2]
    out_square = out_weight.reshape(heads_width // block, block, block).transpose(1, 0, 2)
    first_pack = jnp.concatenate([qkv_weight, out_square.reshape(block, heads_width)], axis=1)
    first_pieces = gather_pair_first(first_pack, 0, VAR)
    first_one = jnp.concatenate(first_pieces, axis=0)
    first_two = from_partner(first_one)
    out_block = first_one[:, width:].reshape(half // block, block, heads_width // block, block)
    out_block = out_block.transpose(2, 1, 0, 3).reshape(heads_width, half)
    out_pieces = gather_pair_first(out_block, 0, TP)
    down_square = down_weight.reshape(ff_local // block, block, block).transpose(1, 0, 2)
    second_pack = jnp.concatenate(
        [gate_up_weight.reshape(block, 2 * ff_local), down_square.reshape(block, ff_local)], axis=1
    )
    weights = gather_pair_first(second_pack, 0, VAR)
    weights = weights + [from_partner(piece) for piece in weights]

    flat_hidden = hidden_in.reshape(row_count, model_width)
    cosine, sine = rotary_tables(full_len)
    columns = normed_blocks(after(place, cosine, sine), flat_hidden)
    head_rows = attention(columns, first_one, first_two, width, cosine, sine)
    head_rows = head_rows.reshape(tp_count, own_rows, heads_width)

    split = 80
    rest = own_rows - split
    heads = lax.all_to_all(head_rows, "tp", split_axis=0, concat_axis=0, tiled=True)
    other_heads = from_partner(heads)
    one, for_partner = project(place, heads, other_heads, [out_pieces])
    two = from_partner(for_partner)
    after_attention, normed_a, normed_b, switch = combine(
        place, run_flat, tp_flat, one, two, flat_hidden, full_len, split
    )

    other_a = lax.ppermute(normed_a, "tp", TP_XL)
    back_b, ahead_b = send_both(normed_b, TP)
    back_a, ahead_a = send_both(normed_a, TP)
    other_back_a, other_ahead_a = send_both(other_a, TP)
    pair = 2 * split
    for_own, for_pair_a, *joined = first_feed_forward(
        [normed_a, other_a, normed_b],
        [[(0, split), (pair, rest)], [(split, split)]],
        weights,
        ff_local,
    )
    far_a = lax.ppermute(after(back_a, for_pair_a), "tp", TP[2])
    other_far_a = lax.ppermute(after(other_ahead_a, for_pair_a), "tp", TP[3])
    far_b = lax.ppermute(after(back_b, for_pair_a), "tp", TP[2])
    in_a = [normed_a, other_a, back_a, other_back_a, ahead_a, other_ahead_a, far_a, other_far_a]
    in_b = [normed_b, back_b, ahead_b, far_b]
    cross_b = cross_each([normed_b] + [after(t, for_pair_a) for t in in_b[1:]], TP)
    for_back, for_ahead, for_back_pair_a, for_ahead_pair_a = feed_forward(
        in_a[2:6] + in_b[1:3],
        [
            [(0, split), (2 * pair, rest)],
            [(pair, split), (2 * pair + rest, rest)],
            [(split, split)],
            [(pair + split, split)],
        ],
        joined,
    )
    for_far, for_far_pair, for_back_pair_b, for_ahead_pair_b, for_pair_b = feed_forward(
        [in_a[6], in_b[3], in_a[7], cross_b[3], cross_b[1], cross_b[2], cross_b[0]],
        [[(0, own_rows)], [(own_rows, own_rows)]]
        + [[(2 * own_rows + k * rest, rest)] for k in range(3)],
        joined,
    )

    for_far_pair = lax.ppermute(for_far_pair, "tp", TP_XL)
    for_far = (for_far.astype(F32) + for_far_pair.astype(F32)).astype(BF)
    whole_terms = [
        for_own,
        lax.ppermute(for_back, "tp", tp_y(3)),
        lax.ppermute(for_ahead, "tp", tp_y(1)),
        lax.ppermute(for_far, "tp", tp_y(2)),
    ]
    terms_a = [term[:split] for term in whole_terms] + [
        lax.ppermute(for_pair_a, "tp", TP_XL),
        lax.ppermute(for_back_pair_a, "tp", tp_y(3, 1)),
        lax.ppermute(for_ahead_pair_a, "tp", tp_y(1, 1)),
    ]
    terms_b = [term[split:] for term in whole_terms] + [
        lax.ppermute(for_back_pair_b, "tp", tp_y(3, 1)),
        lax.ppermute(for_ahead_pair_b, "tp", tp_y(1, 1)),
        lax.ppermute(for_pair_b, "tp", TP_XL),
    ]

    def finished(rows, terms):
        mlp = sum(term.astype(F32) for term in terms)
        return (after_attention[rows].astype(F32) + switch[rows, :1] * mlp).astype(BF)

    result_a = finished(slice(0, split), terms_a)
    result_b = finished(slice(split, own_rows), terms_b)

    parts_a = gather_each(result_a, TP)
    parts_b = gather_ring(result_b, TP)
    cross = cross_each(parts_b, TP)
    shape = (tp_count, own_rows, model_width)
    pieces = parts_a[:6] + parts_b
    items = [(16 + k, 0) for k in range(6)]
    items += [(24 + k, split) for k in range(4)]
    gathered = place_pieces(place, pieces, items, shape)
    items = [(22, 0), (23, 0)] + [(28 + k, split) for k in range(4)]
    gathered = place_pieces(place, parts_a[6:] + cross, items, shape, gathered)
    return gathered.reshape(seq_count, full_len, model_width)


def solution(mesh):
    return jax.shard_map(
        layer,
        mesh=mesh,
        in_specs=(
            P("var", None, None),
            P("var", None),
            P("var", "tp"),
            P("tp", "var"),
            P("var", None, "tp"),
            P("tp", "var"),
        ),
        out_specs=P("var", None, None),
        check_vma=False,
    )
```

profile of v0, /device:TPU:0, one launch (start us, length us, event | category | flops | bytes accessed | tf_op | source)
XLA Modules:
  0.0 287.8 jit_solution(4234503097532356537)
XLA Ops:
  3.1 3.1 %collective-permute-start = (bf16[128,640]{1,0:T(8,128)(2,1)S(1)}, bf16[128,640]{1,0:T(8,128)(2,1)S(1)}, u32[]{:S(2)}, u32[]{:S(2)}) collective-permute-start(bf16[128,640]{1,0:T(8,128)(2,1)S(1)} %get-tuple-element.59), channel_id=1, source_target_pairs={{0,64},{8,72},{16,80},{24,88},{32,96},{40,104},{48,112},{56,120},{... | collective-permute-start | bytes 491528 | tf_op jit(solution)/shard_map/ppermute | solution.py:42
  15.0 3.1 %collective-permute-start.13 = (bf16[128,3072]{1,0:T(8,128)(2,1)S(1)}, bf16[128,3072]{1,0:T(8,128)(2,1)S(1)}, u32[]{:S(2)}, u32[]{:S(2)}) collective-permute-start(bf16[128,3072]{1,0:T(8,128)(2,1)S(1)} %bitcast_dynamic-update-slice_fusion), channel_id=1, source_target_pairs={{0,64},{8,72},{16,80},{24,88},{32,96},{40,104},{48,112},{56,120},{... | collective-permute-start | bytes 2359304 | tf_op jit(solution)/shard_map/ppermute | solution.py:42
  21.8 3.3 %collective-permute-start.4 = (bf16[128,640]{1,0:T(8,128)(2,1)S(1)}, bf16[128,640]{1,0:T(8,128)(2,1)S(1)}, u32[]{:S(2)}, u32[]{:S(2)}) collective-permute-start(bf16[128,640]{1,0:T(8,128)(2,1)S(1)} %split.25), channel_id=1, source_target_pairs={{0,48},{8,56},{16,0},{24,8},{32,16},{40,24},{48,32},{56,40},{64,11... | collective-permute-start | bytes 491528 | tf_op jit(solution)/shard_map/ppermute | solution.py:47
  34.9 3.2 %collective-permute-start.15 = (bf16[256,3072]{1,0:T(8,128)(2,1)S(1)}, bf16[256,3072]{1,0:T(8,128)(2,1)}, u32[]{:S(2)}, u32[]{:S(2)}) collective-permute-start(bf16[256,3072]{1,0:T(8,128)(2,1)S(1)} %pad_maximum_fusion.refs_0_.refs_10_.refs_20_), channel_id=1, source_target_pairs={{0,48},{8,56},{16,0},{24,8},{32,16},{40,24},{48,32},{56,40},{64,11... | collective-permute-start | bytes 4718600 | tf_op jit(solution)/shard_map/ppermute | solution.py:44
  39.0 7.3 %collective-permute-done.7 = bf16[256,1024]{1,0:T(8,128)(2,1)S(1)} collective-permute-done((bf16[256,1024]{1,0:T(8,128)(2,1)S(1)}, bf16[256,1024]{1,0:T(8,128)(2,1)S(1)}, u32[]{:S(2)}, u32[]{:S(2)}) %collective-permute-start.7) | collective-permute-done | bytes 524320 | tf_op jit(solution)/shard_map/ppermute | solution.py:42
  51.9 7.3 %normed_blocks.1.rows_ref = bf16[1152,2048]{1,0:T(8,128)(2,1)} custom-call(s32[32]{0:T(128)} %compare_select_fusion.3.place_ref, bf16[1152,2048]{1,0:T(8,128)(2,1)} %bitcast.25), custom_call_target="tpu_custom_call" | custom-call | flops 9437184 | bytes 9437184 | tf_op jit(solution)/shard_map/normed_blocks/pallas_call | solution.py:108
  59.2 11.6 %attention.1 = bf16[1152,256]{1,0:T(8,128)(2,1)} custom-call(bf16[1152,2048]{1,0:T(8,128)(2,1)} %normed_blocks.1.rows_ref, bf16[1024,640]{1,0:T(8,128)(2,1)} %constant_dynamic-update-slice_fusion.1.one_ref, bf16[1024,640]{1,0:T(8,128)(2,1)} %collective-permute-done.5.two_ref, f32[384,128]{1,0:T(8,128)} %get-tuple-element.62.cosine_ref, ...), custom_call_target="tpu_custom_call" | custom-call | flops 2264924160 | bytes 6291456 | tf_op jit(solution)/shard_map/attention/pallas_call | solution.py:458
  70.8 14.4 %all_to_all.5.own_ref = bf16[8,144,256]{2,1,0:T(8,128)(2,1)S(1)} all-to-all(bf16[8,144,256]{2,1,0:T(8,128)(2,1)} %bitcast.31), channel_id=1, replica_groups=mesh['var'=16,'tp'=8] {'tp'}, dimensions={0} | all-to-all | bytes 1179648 | tf_op jit(solution)/shard_map/all_to_all | solution.py:526
  91.5 9.4 %collective-permute-done.10.refs_3_ = bf16[256,1024]{1,0:T(8,128)(2,1)S(1)} collective-permute-done((bf16[256,1024]{1,0:T(8,128)(2,1)S(1)}, bf16[256,1024]{1,0:T(8,128)(2,1)S(1)}, u32[]{:S(2)}, u32[]{:S(2)}) %collective-permute-start.10) | collective-permute-done | bytes 524320 | tf_op jit(solution)/shard_map/ppermute | solution.py:46
  105.1 5.4 %project.1 = (f32[144,1024]{1,0:T(8,128)}, bf16[144,1024]{1,0:T(8,128)(2,1)}) custom-call(s32[32]{0:T(128)} %compare_select_fusion.3.place_ref, bf16[8,144,256]{2,1,0:T(8,128)(2,1)} %copy-done.2, bf16[8,144,256]{2,1,0:T(8,128)(2,1)} %copy-done.9, bf16[512,1024]{1,0:T(8,128)(2,1)} %constant_dynamic-update-slice_fusion.7.refs_0_, bf16[512,1024]{1,0:T(8,128)(2,1)} %copy-done.3, ...), custom_call_target="tpu_custom_call" | custom-call | flops 1207959552 | bytes 4194304 | tf_op jit(solution)/shard_map/project/pallas_call | solution.py:162
  111.2 8.9 %collective-permute-done.17.refs_4_.refs_14_.refs_24_ = bf16[128,3072]{1,0:T(8,128)(2,1)} collective-permute-done((bf16[128,3072]{1,0:T(8,128)(2,1)S(1)}, bf16[128,3072]{1,0:T(8,128)(2,1)}, u32[]{:S(2)}, u32[]{:S(2)}) %collective-permute-start.17) | collective-permute-done | bytes 786464 | tf_op jit(solution)/shard_map/ppermute | solution.py:47
  121.4 3.5 %combine.1 = (bf16[144,2048]{1,0:T(8,128)(2,1)}, bf16[80,2048]{1,0:T(8,128)(2,1)}, bf16[64,2048]{1,0:T(8,128)(2,1)}, f32[144,128]{1,0:T(8,128)}) custom-call(s32[32]{0:T(128)} %compare_select_fusion.3.place_ref, s32[6]{0:T(128)} %reshape.60.run_ref, s32[1]{0:T(128)} %bitcast.tp_ref, f32[144,1024]{1,0:T(8,128)} %get-tuple-element.32.one_ref, ...), custom_call_target="tpu_custom_call" | custom-call | flops 2359296 | bytes 3538944 | tf_op jit(solution)/shard_map/combine/pallas_call | solution.py:207
  125.7 9.2 %collective-permute-done.23.refs_31_ = bf16[80,2048]{1,0:T(8,128)(2,1)S(1)} collective-permute-done((bf16[80,2048]{1,0:T(8,128)(2,1)}, bf16[80,2048]{1,0:T(8,128)(2,1)S(1)}, u32[]{:S(2)}, u32[]{:S(2)}) %collective-permute-start.23) | collective-permute-done | bytes 327712 | tf_op jit(solution)/shard_map/ppermute | solution.py:534
  137.0 3.2 %collective-permute-start.27 = (bf16[80,2048]{1,0:T(8,128)(2,1)S(1)}, bf16[80,2048]{1,0:T(8,128)(2,1)S(1)}, u32[]{:S(2)}, u32[]{:S(2)}) collective-permute-start(bf16[80,2048]{1,0:T(8,128)(2,1)S(1)} %collective-permute-done.23.refs_31_), channel_id=1, source_target_pairs={{0,6},{1,7},{2,0},{3,1},{4,2},{5,3},{6,4},{7,5},{8,14},{9,15},{10,... | collective-permute-start | bytes 983048 | tf_op jit(solution)/shard_map/ppermute | solution.py:53
  140.1 11.9 %first_feed_forward.1 = (bf16[144,2048]{1,0:T(8,128)(2,1)}, bf16[80,2048]{1,0:T(8,128)(2,1)}, bf16[2048,1024]{1,0:T(8,128)(2,1)}, bf16[2048,1024]{1,0:T(8,128)(2,1)}, bf16[1024,2048]{1,0:T(8,128)(2,1)}) custom-call(bf16[256,3072]{1,0:T(8,128)(2,1)} %copy-done, bf16[256,3072]{1,0:T(8,128)(2,1)} %copy-done.1, ...), custom_call_target="tpu_custom_call" | custom-call | flops 2818572288 | bytes 14417920 | tf_op jit(solution)/shard_map/first_feed_forward/pallas_call | solution.py:316
  153.0 3.2 %collective-permute-start.34 = (bf16[80,2048]{1,0:T(8,128)(2,1)S(1)}, bf16[80,2048]{1,0:T(8,128)(2,1)S(1)}, u32[]{:S(2)}, u32[]{:S(2)}) collective-permute-start(bf16[80,2048]{1,0:T(8,128)(2,1)S(1)} %collective-permute-done.27.refs_3_), channel_id=1, source_target_pairs={{0,6},{1,7},{2,0},{3,1},{4,2},{5,3},{6,4},{7,5},{8,14},{9,15},{10,... | collective-permute-start | bytes 983048 | tf_op jit(solution)/shard_map/ppermute | solution.py:546
  157.5 5.0 %collective-permute-done.33.refs_1_ = bf16[64,2048]{1,0:T(8,128)(2,1)S(1)} collective-permute-done((bf16[64,2048]{1,0:T(8,128)(2,1)S(1)}, bf16[64,2048]{1,0:T(8,128)(2,1)S(1)}, u32[]{:S(2)}, u32[]{:S(2)}) %collective-permute-start.33) | collective-permute-done | bytes 262176 | tf_op jit(solution)/shard_map/ppermute | solution.py:547
  166.7 3.4 %collective-permute-start.26 = (bf16[80,2048]{1,0:T(8,128)(2,1)S(1)}, bf16[80,2048]{1,0:T(8,128)(2,1)S(1)}, u32[]{:S(2)}, u32[]{:S(2)}) collective-permute-start(bf16[80,2048]{1,0:T(8,128)(2,1)S(1)} %copy-done.12), channel_id=1, source_target_pairs={{0,6},{1,7},{2,0},{3,1},{4,2},{5,3},{6,4},{7,5},{8,14},{9,15},{10,... | collective-permute-start | bytes 983048 | tf_op jit(solution)/shard_map/ppermute | solution.py:53
  176.1 11.8 %feed_forward.3 = (bf16[144,2048]{1,0:T(8,128)(2,1)}, bf16[144,2048]{1,0:T(8,128)(2,1)}, bf16[64,2048]{1,0:T(8,128)(2,1)}, bf16[64,2048]{1,0:T(8,128)(2,1)}, bf16[64,2048]{1,0:T(8,128)(2,1)}) custom-call(bf16[2048,1024]{1,0:T(8,128)(2,1)} %get-tuple-element.39.gate_ref, bf16[2048,1024]{1,0:T(8,128)(2,1)} %get-tuple-element.40.up_ref, ...), custom_call_target="tpu_custom_call" | custom-call | flops 6039797760 | bytes 16515072 | tf_op jit(solution)/shard_map/feed_forward/pallas_call | solution.py:337
  191.6 11.6 %feed_forward.2 = (bf16[144,2048]{1,0:T(8,128)(2,1)}, bf16[144,2048]{1,0:T(8,128)(2,1)}, bf16[80,2048]{1,0:T(8,128)(2,1)}, bf16[80,2048]{1,0:T(8,128)(2,1)}) custom-call(bf16[2048,1024]{1,0:T(8,128)(2,1)} %get-tuple-element.39.gate_ref, bf16[2048,1024]{1,0:T(8,128)(2,1)} %get-tuple-element.40.up_ref, bf16[1024,2048]{1,0:T(8,128)(2,1)} %get-tuple-element.41.down_ref, ...), custom_call_target="tpu_custom_call" | custom-call | flops 5637144576 | bytes 16252928 | tf_op jit(solution)/shard_map/feed_forward/pallas_call | solution.py:337
  211.0 8.6 %collective-permute-done.42 = bf16[80,2048]{1,0:T(8,128)(2,1)S(1)} collective-permute-done((bf16[80,2048]{1,0:T(8,128)(2,1)}, bf16[80,2048]{1,0:T(8,128)(2,1)S(1)}, u32[]{:S(2)}, u32[]{:S(2)}) %collective-permute-start.42) | collective-permute-done | bytes 327712 | tf_op jit(solution)/shard_map/ppermute | solution.py:578
  219.6 3.1 %collective-permute-start.49 = (bf16[64,2048]{1,0:T(8,128)(2,1)S(1)}, bf16[64,2048]{1,0:T(8,128)(2,1)S(1)}, u32[]{:S(2)}, u32[]{:S(2)}) collective-permute-start(bf16[64,2048]{1,0:T(8,128)(2,1)S(1)} %copy-done.47), channel_id=1, source_target_pairs={{0,7},{1,6},{2,1},{3,0},{4,3},{5,2},{6,5},{7,4},{8,15},{9,14},{10,... | collective-permute-start | bytes 786440 | tf_op jit(solution)/shard_map/ppermute | solution.py:582
  222.7 4.4 %collective-permute-done.43 = bf16[80,2048]{1,0:T(8,128)(2,1)S(1)} collective-permute-done((bf16[80,2048]{1,0:T(8,128)(2,1)S(1)}, bf16[80,2048]{1,0:T(8,128)(2,1)S(1)}, u32[]{:S(2)}, u32[]{:S(2)}) %collective-permute-start.43) | collective-permute-done | bytes 327712 | tf_op jit(solution)/shard_map/ppermute | solution.py:579
  228.6 12.2 %collective-permute-done.30 = bf16[144,2048]{1,0:T(8,128)(2,1)S(1)} collective-permute-done((bf16[144,2048]{1,0:T(8,128)(2,1)}, bf16[144,2048]{1,0:T(8,128)(2,1)S(1)}, u32[]{:S(2)}, u32[]{:S(2)}) %collective-permute-start.30) | collective-permute-done | bytes 589856 | tf_op jit(solution)/shard_map/ppermute | solution.py:572
  240.9 4.0 %collective-permute-done.31 = bf16[144,2048]{1,0:T(8,128)(2,1)S(1)} collective-permute-done((bf16[144,2048]{1,0:T(8,128)(2,1)}, bf16[144,2048]{1,0:T(8,128)(2,1)S(1)}, u32[]{:S(2)}, u32[]{:S(2)}) %collective-permute-start.31) | collective-permute-done | bytes 589856 | tf_op jit(solution)/shard_map/ppermute | solution.py:573
  246.3 3.3 %collective-permute-done.51 = bf16[64,2048]{1,0:T(8,128)(2,1)S(1)} collective-permute-done((bf16[64,2048]{1,0:T(8,128)(2,1)S(1)}, bf16[64,2048]{1,0:T(8,128)(2,1)S(1)}, u32[]{:S(2)}, u32[]{:S(2)}) %collective-permute-start.51) | collective-permute-done | bytes 262176 | tf_op jit(solution)/shard_map/ppermute | solution.py:584
  250.1 3.2 %collective-permute-start.55 = (bf16[64,2048]{1,0:T(8,128)(2,1)S(1)}, bf16[64,2048]{1,0:T(8,128)(2,1)S(1)}, u32[]{:S(2)}, u32[]{:S(2)}) collective-permute-start(bf16[64,2048]{1,0:T(8,128)(2,1)S(1)} %add_convert_fusion.2.refs_6_), channel_id=1, source_target_pairs={{0,6},{1,7},{2,0},{3,1},{4,2},{5,3},{6,4},{7,5},{8,14},{9,15},{10,... | collective-permute-start | bytes 786440 | tf_op jit(solution)/shard_map/ppermute | solution.py:71
  254.5 3.2 %collective-permute-start.47 = (bf16[80,2048]{1,0:T(8,128)(2,1)S(1)}, bf16[80,2048]{1,0:T(8,128)(2,1)S(1)}, u32[]{:S(2)}, u32[]{:S(2)}) collective-permute-start(bf16[80,2048]{1,0:T(8,128)(2,1)S(1)} %collective-permute-done.46.refs_1_), channel_id=1, source_target_pairs={{0,6},{1,7},{2,0},{3,1},{4,2},{5,3},{6,4},{7,5},{8,14},{9,15},{10,... | collective-permute-start | bytes 983048 | tf_op jit(solution)/shard_map/ppermute | solution.py:62
  263.3 4.0 %collective-permute-done.44.refs_2_ = bf16[80,2048]{1,0:T(8,128)(2,1)S(1)} collective-permute-done((bf16[80,2048]{1,0:T(8,128)(2,1)S(1)}, bf16[80,2048]{1,0:T(8,128)(2,1)S(1)}, u32[]{:S(2)}, u32[]{:S(2)}) %collective-permute-start.44) | collective-permute-done | bytes 327712 | tf_op jit(solution)/shard_map/ppermute | solution.py:59
  267.4 3.2 %collective-permute-start.48 = (bf16[80,2048]{1,0:T(8,128)(2,1)S(1)}, bf16[80,2048]{1,0:T(8,128)(2,1)S(1)}, u32[]{:S(2)}, u32[]{:S(2)}) collective-permute-start(bf16[80,2048]{1,0:T(8,128)(2,1)S(1)} %collective-permute-done.47.refs_5_), channel_id=1, source_target_pairs={{0,6},{1,7},{2,0},{3,1},{4,2},{5,3},{6,4},{7,5},{8,14},{9,15},{10,... | collective-permute-start | bytes 983048 | tf_op jit(solution)/shard_map/ppermute | solution.py:64
  275.8 4.2 %place_pieces.2.refs_6_ = bf16[8,144,2048]{2,1,0:T(8,128)(2,1)} custom-call(s32[32]{0:T(128)} %compare_select_fusion.3.place_ref, bf16[80,2048]{1,0:T(8,128)(2,1)} %copy-done.4, bf16[80,2048]{1,0:T(8,128)(2,1)} %copy-done.14, bf16[80,2048]{1,0:T(8,128)(2,1)} %copy-done.16, bf16[80,2048]{1,0:T(8,128)(2,1)} %copy-done.20, bf16[80,2048]{1,0:T(8,128)(2,1)} %copy-done.18, ...), custom_call_target="tpu_custom_call" | custom-call | bytes 6029312 | tf_op jit(solution)/shard_map/place_pieces/pallas_call | solution.py:371
  284.3 3.4 %place_pieces.3 = bf16[8,144,2048]{2,1,0:T(8,128)(2,1)} custom-call(s32[32]{0:T(128)} %compare_select_fusion.3.place_ref, bf16[80,2048]{1,0:T(8,128)(2,1)} %copy-done.17, bf16[80,2048]{1,0:T(8,128)(2,1)} %copy-done.19, bf16[64,2048]{1,0:T(8,128)(2,1)} %copy-done.23, bf16[64,2048]{1,0:T(8,128)(2,1)} %copy-done.27, ...), custom_call_target="tpu_custom_call", output_to_operand_aliasing={{}: (7, {})} | custom-call | bytes 3407872 | tf_op jit(solution)/shard_map/place_pieces/pallas_call | solution.py:371
  (242 shorter events, 90.2 us)
Async XLA Ops:
  15.0 19.7 %collective-permute-start.13 = (bf16[128,3072]{1,0:T(8,128)(2,1)S(1)}, bf16[128,3072]{1,0:T(8,128)(2,1)S(1)}, u32[]{:S(2)}, u32[]{:S(2)}) collective-permute-start(bf16[128,3072]{1,0:T(8,128)(2,1)S(1)} %bitcast_dynamic-update-slice_fusion), channel_id=1, source_target_pairs={{0,64},{8,72},{16,80},{24,88},{32,96},{40,104},{48,112},{56,120},{... | collective-permute-start | bytes 2359304 | tf_op jit(solution)/shard_map/ppermute | solution.py:42
  29.7 29.6 %collective-permute-start.5 = (bf16[1024,640]{1,0:T(8,128)(2,1)}, bf16[1024,640]{1,0:T(8,128)(2,1)}, u32[]{:S(2)}, u32[]{:S(2)}) collective-permute-start(bf16[1024,640]{1,0:T(8,128)(2,1)} %constant_dynamic-update-slice_fusion.1.one_ref), channel_id=1, source_target_pairs={{0,8},{8,0},{16,24},{24,16},{32,40},{40,32},{48,56},{56,48},{64,72... | collective-permute-start | bytes 3932168 | tf_op jit(solution)/shard_map/ppermute | solution.py:497
  34.8 54.9 %collective-permute-start.14 = (bf16[256,3072]{1,0:T(8,128)(2,1)S(1)}, bf16[256,3072]{1,0:T(8,128)(2,1)S(1)}, u32[]{:S(2)}, u32[]{:S(2)}) collective-permute-start(bf16[256,3072]{1,0:T(8,128)(2,1)S(1)} %pad_maximum_fusion.refs_0_.refs_10_.refs_20_), channel_id=1, source_target_pairs={{0,16},{8,24},{16,32},{24,40},{32,48},{40,56},{48,0},{56,8},{64,80... | collective-permute-start | bytes 4718600 | tf_op jit(solution)/shard_map/ppermute | solution.py:43
  34.9 55.0 %collective-permute-start.15 = (bf16[256,3072]{1,0:T(8,128)(2,1)S(1)}, bf16[256,3072]{1,0:T(8,128)(2,1)}, u32[]{:S(2)}, u32[]{:S(2)}) collective-permute-start(bf16[256,3072]{1,0:T(8,128)(2,1)S(1)} %pad_maximum_fusion.refs_0_.refs_10_.refs_20_), channel_id=1, source_target_pairs={{0,48},{8,56},{16,0},{24,8},{32,16},{40,24},{48,32},{56,40},{64,11... | collective-permute-start | bytes 4718600 | tf_op jit(solution)/shard_map/ppermute | solution.py:44
  47.2 38.0 %collective-permute-start.8 = (bf16[512,1024]{1,0:T(8,128)(2,1)}, bf16[512,1024]{1,0:T(8,128)(2,1)S(1)}, u32[]{:S(2)}, u32[]{:S(2)}) collective-permute-start(bf16[512,1024]{1,0:T(8,128)(2,1)} %constant_dynamic-update-slice_fusion.7.refs_0_), channel_id=1, source_target_pairs={{0,2},{1,3},{2,4},{3,5},{4,6},{5,7},{6,0},{7,1},{8,10},{9,11},{10,... | collective-permute-start | bytes 3145736 | tf_op jit(solution)/shard_map/ppermute | solution.py:43
  48.7 37.2 %collective-permute-start.9 = (bf16[512,1024]{1,0:T(8,128)(2,1)}, bf16[512,1024]{1,0:T(8,128)(2,1)}, u32[]{:S(2)}, u32[]{:S(2)}) collective-permute-start(bf16[512,1024]{1,0:T(8,128)(2,1)} %constant_dynamic-update-slice_fusion.7.refs_0_), channel_id=1, source_target_pairs={{0,6},{1,7},{2,0},{3,1},{4,2},{5,3},{6,4},{7,5},{8,14},{9,15},{10,... | collective-permute-start | bytes 3145736 | tf_op jit(solution)/shard_map/ppermute | solution.py:44
  85.2 18.4 %collective-permute-start.6 = (bf16[8,144,256]{2,1,0:T(8,128)(2,1)S(1)}, bf16[8,144,256]{2,1,0:T(8,128)(2,1)S(1)}, u32[]{:S(2)}, u32[]{:S(2)}) collective-permute-start(bf16[8,144,256]{2,1,0:T(8,128)(2,1)S(1)} %all_to_all.5.own_ref), channel_id=1, source_target_pairs={{0,8},{8,0},{16,24},{24,16},{32,40},{40,32},{48,56},{56,48},{64,72... | collective-permute-start | bytes 1769480 | tf_op jit(solution)/shard_map/ppermute | solution.py:497
  85.3 15.6 %collective-permute-start.10 = (bf16[256,1024]{1,0:T(8,128)(2,1)S(1)}, bf16[256,1024]{1,0:T(8,128)(2,1)S(1)}, u32[]{:S(2)}, u32[]{:S(2)}) collective-permute-start(bf16[256,1024]{1,0:T(8,128)(2,1)S(1)} %split.26), channel_id=1, source_target_pairs={{0,2},{1,3},{2,4},{3,5},{4,6},{5,7},{6,0},{7,1},{8,10},{9,11},{10,... | collective-permute-start | bytes 1572872 | tf_op jit(solution)/shard_map/ppermute | solution.py:46
  87.0 16.5 %collective-permute-start.11 = (bf16[256,1024]{1,0:T(8,128)(2,1)S(1)}, bf16[256,1024]{1,0:T(8,128)(2,1)S(1)}, u32[]{:S(2)}, u32[]{:S(2)}) collective-permute-start(bf16[256,1024]{1,0:T(8,128)(2,1)S(1)} %split.27), channel_id=1, source_target_pairs={{0,6},{1,7},{2,0},{3,1},{4,2},{5,3},{6,4},{7,5},{8,14},{9,15},{10,... | collective-permute-start | bytes 1572872 | tf_op jit(solution)/shard_map/ppermute | solution.py:47
  89.7 35.2 %collective-permute-start.18 = (bf16[256,3072]{1,0:T(8,128)(2,1)S(1)}, bf16[256,3072]{1,0:T(8,128)(2,1)}, u32[]{:S(2)}, u32[]{:S(2)}) collective-permute-start(bf16[256,3072]{1,0:T(8,128)(2,1)S(1)} %pad_maximum_fusion.refs_0_.refs_10_.refs_20_), channel_id=1, source_target_pairs={{0,8},{8,0},{16,24},{24,16},{32,40},{40,32},{48,56},{56,48},{64,72... | collective-permute-start | bytes 4718600 | tf_op jit(solution)/shard_map/ppermute | solution.py:497
  89.9 21.3 %collective-permute-start.16 = (bf16[128,3072]{1,0:T(8,128)(2,1)S(1)}, bf16[128,3072]{1,0:T(8,128)(2,1)}, u32[]{:S(2)}, u32[]{:S(2)}) collective-permute-start(bf16[128,3072]{1,0:T(8,128)(2,1)S(1)} %split.28), channel_id=1, source_target_pairs={{0,16},{8,24},{16,32},{24,40},{32,48},{40,56},{48,0},{56,8},{64,80... | collective-permute-start | bytes 2359304 | tf_op jit(solution)/shard_map/ppermute | solution.py:46
  100.9 19.3 %collective-permute-start.17 = (bf16[128,3072]{1,0:T(8,128)(2,1)S(1)}, bf16[128,3072]{1,0:T(8,128)(2,1)}, u32[]{:S(2)}, u32[]{:S(2)}) collective-permute-start(bf16[128,3072]{1,0:T(8,128)(2,1)S(1)} %split.29), channel_id=1, source_target_pairs={{0,48},{8,56},{16,0},{24,8},{32,16},{40,24},{48,32},{56,40},{64,11... | collective-permute-start | bytes 2359304 | tf_op jit(solution)/shard_map/ppermute | solution.py:47
  103.5 33.4 %collective-permute-start.19 = (bf16[256,3072]{1,0:T(8,128)(2,1)S(1)}, bf16[256,3072]{1,0:T(8,128)(2,1)}, u32[]{:S(2)}, u32[]{:S(2)}) collective-permute-start(bf16[256,3072]{1,0:T(8,128)(2,1)S(1)} %collective-permute-done.14.refs_1_.refs_11_.refs_21_), channel_id=1, source_target_pairs={{0,8},{8,0},{16,24},{24,16},{32,40},{40,32},{48,56},{56,48},{64,72... | collective-permute-start | bytes 4718600 | tf_op jit(solution)/shard_map/ppermute | solution.py:497
  105.1 35.0 %collective-permute-start.20 = (bf16[256,3072]{1,0:T(8,128)(2,1)}, bf16[256,3072]{1,0:T(8,128)(2,1)}, u32[]{:S(2)}, u32[]{:S(2)}) collective-permute-start(bf16[256,3072]{1,0:T(8,128)(2,1)} %collective-permute-done.15.refs_2_.refs_12_.refs_22_), channel_id=1, source_target_pairs={{0,8},{8,0},{16,24},{24,16},{32,40},{40,32},{48,56},{56,48},{64,72... | collective-permute-start | bytes 4718600 | tf_op jit(solution)/shard_map/ppermute | solution.py:497
  120.2 16.7 %collective-permute-start.22 = (bf16[128,3072]{1,0:T(8,128)(2,1)}, bf16[128,3072]{1,0:T(8,128)(2,1)}, u32[]{:S(2)}, u32[]{:S(2)}) collective-permute-start(bf16[128,3072]{1,0:T(8,128)(2,1)} %collective-permute-done.17.refs_4_.refs_14_.refs_24_), channel_id=1, source_target_pairs={{0,8},{8,0},{16,24},{24,16},{32,40},{40,32},{48,56},{56,48},{64,72... | collective-permute-start | bytes 2359304 | tf_op jit(solution)/shard_map/ppermute | solution.py:497
  134.9 21.3 %collective-permute-start.29 = (bf16[64,2048]{1,0:T(8,128)(2,1)}, bf16[64,2048]{1,0:T(8,128)(2,1)S(1)}, u32[]{:S(2)}, u32[]{:S(2)}) collective-permute-start(bf16[64,2048]{1,0:T(8,128)(2,1)} %get-tuple-element.37.refs_32_), channel_id=1, source_target_pairs={{0,6},{1,7},{2,0},{3,1},{4,2},{5,3},{6,4},{7,5},{8,14},{9,15},{10,... | collective-permute-start | bytes 786440 | tf_op jit(solution)/shard_map/ppermute | solution.py:53
  134.9 17.1 %collective-permute-start.28 = (bf16[64,2048]{1,0:T(8,128)(2,1)}, bf16[64,2048]{1,0:T(8,128)(2,1)S(1)}, u32[]{:S(2)}, u32[]{:S(2)}) collective-permute-start(bf16[64,2048]{1,0:T(8,128)(2,1)} %get-tuple-element.37.refs_32_), channel_id=1, source_target_pairs={{0,2},{1,3},{2,4},{3,5},{4,6},{5,7},{6,0},{7,1},{8,10},{9,11},{10,... | collective-permute-start | bytes 786440 | tf_op jit(solution)/shard_map/ppermute | solution.py:53
  136.9 16.0 %collective-permute-start.24 = (bf16[80,2048]{1,0:T(8,128)(2,1)}, bf16[80,2048]{1,0:T(8,128)(2,1)S(1)}, u32[]{:S(2)}, u32[]{:S(2)}) collective-permute-start(bf16[80,2048]{1,0:T(8,128)(2,1)} %get-tuple-element.36.refs_30_), channel_id=1, source_target_pairs={{0,2},{1,3},{2,4},{3,5},{4,6},{5,7},{6,0},{7,1},{8,10},{9,11},{10,... | collective-permute-start | bytes 983048 | tf_op jit(solution)/shard_map/ppermute | solution.py:53
  137.0 16.0 %collective-permute-start.27 = (bf16[80,2048]{1,0:T(8,128)(2,1)S(1)}, bf16[80,2048]{1,0:T(8,128)(2,1)S(1)}, u32[]{:S(2)}, u32[]{:S(2)}) collective-permute-start(bf16[80,2048]{1,0:T(8,128)(2,1)S(1)} %collective-permute-done.23.refs_31_), channel_id=1, source_target_pairs={{0,6},{1,7},{2,0},{3,1},{4,2},{5,3},{6,4},{7,5},{8,14},{9,15},{10,... | collective-permute-start | bytes 983048 | tf_op jit(solution)/shard_map/ppermute | solution.py:53
  152.9 19.4 %collective-permute-start.32 = (bf16[80,2048]{1,0:T(8,128)(2,1)S(1)}, bf16[80,2048]{1,0:T(8,128)(2,1)S(1)}, u32[]{:S(2)}, u32[]{:S(2)}) collective-permute-start(bf16[80,2048]{1,0:T(8,128)(2,1)S(1)} %collective-permute-done.24.refs_0_), channel_id=1, source_target_pairs={{0,2},{1,3},{2,4},{3,5},{4,6},{5,7},{6,0},{7,1},{8,10},{9,11},{10,... | collective-permute-start | bytes 983048 | tf_op jit(solution)/shard_map/ppermute | solution.py:545
  153.0 19.4 %collective-permute-start.34 = (bf16[80,2048]{1,0:T(8,128)(2,1)S(1)}, bf16[80,2048]{1,0:T(8,128)(2,1)S(1)}, u32[]{:S(2)}, u32[]{:S(2)}) collective-permute-start(bf16[80,2048]{1,0:T(8,128)(2,1)S(1)} %collective-permute-done.27.refs_3_), channel_id=1, source_target_pairs={{0,6},{1,7},{2,0},{3,1},{4,2},{5,3},{6,4},{7,5},{8,14},{9,15},{10,... | collective-permute-start | bytes 983048 | tf_op jit(solution)/shard_map/ppermute | solution.py:546
  166.7 23.4 %collective-permute-start.26 = (bf16[80,2048]{1,0:T(8,128)(2,1)S(1)}, bf16[80,2048]{1,0:T(8,128)(2,1)S(1)}, u32[]{:S(2)}, u32[]{:S(2)}) collective-permute-start(bf16[80,2048]{1,0:T(8,128)(2,1)S(1)} %copy-done.12), channel_id=1, source_target_pairs={{0,6},{1,7},{2,0},{3,1},{4,2},{5,3},{6,4},{7,5},{8,14},{9,15},{10,... | collective-permute-start | bytes 983048 | tf_op jit(solution)/shard_map/ppermute | solution.py:53
  172.3 17.8 %collective-permute-start.25 = (bf16[80,2048]{1,0:T(8,128)(2,1)}, bf16[80,2048]{1,0:T(8,128)(2,1)S(1)}, u32[]{:S(2)}, u32[]{:S(2)}) collective-permute-start(bf16[80,2048]{1,0:T(8,128)(2,1)} %copy-done.13), channel_id=1, source_target_pairs={{0,2},{1,3},{2,4},{3,5},{4,6},{5,7},{6,0},{7,1},{8,10},{9,11},{10,... | collective-permute-start | bytes 983048 | tf_op jit(solution)/shard_map/ppermute | solution.py:53
  188.0 18.1 %collective-permute-start.39 = (bf16[144,2048]{1,0:T(8,128)(2,1)}, bf16[144,2048]{1,0:T(8,128)(2,1)S(1)}, u32[]{:S(2)}, u32[]{:S(2)}) collective-permute-start(bf16[144,2048]{1,0:T(8,128)(2,1)} %get-tuple-element.51), channel_id=1, source_target_pairs={{0,1},{1,0},{2,3},{3,2},{4,5},{5,4},{6,7},{7,6},{8,9},{9,8},{10,11... | collective-permute-start | bytes 1769480 | tf_op jit(solution)/shard_map/ppermute | solution.py:568
  188.8 21.0 %collective-permute-start.41 = (bf16[80,2048]{1,0:T(8,128)(2,1)S(1)}, bf16[80,2048]{1,0:T(8,128)(2,1)S(1)}, u32[]{:S(2)}, u32[]{:S(2)}) collective-permute-start(bf16[80,2048]{1,0:T(8,128)(2,1)S(1)} %copy-done.35), channel_id=1, source_target_pairs={{0,1},{1,0},{2,3},{3,2},{4,5},{5,4},{6,7},{7,6},{8,9},{9,8},{10,11... | collective-permute-start | bytes 983048 | tf_op jit(solution)/shard_map/ppermute | solution.py:577
  203.2 37.7 %collective-permute-start.30 = (bf16[144,2048]{1,0:T(8,128)(2,1)}, bf16[144,2048]{1,0:T(8,128)(2,1)S(1)}, u32[]{:S(2)}, u32[]{:S(2)}) collective-permute-start(bf16[144,2048]{1,0:T(8,128)(2,1)} %get-tuple-element.42), channel_id=1, source_target_pairs={{0,6},{1,7},{2,0},{3,1},{4,2},{5,3},{6,4},{7,5},{8,14},{9,15},{10,... | collective-permute-start | bytes 1769480 | tf_op jit(solution)/shard_map/ppermute | solution.py:572
  206.1 38.8 %collective-permute-start.31 = (bf16[144,2048]{1,0:T(8,128)(2,1)}, bf16[144,2048]{1,0:T(8,128)(2,1)S(1)}, u32[]{:S(2)}, u32[]{:S(2)}) collective-permute-start(bf16[144,2048]{1,0:T(8,128)(2,1)} %get-tuple-element.43), channel_id=1, source_target_pairs={{0,2},{1,3},{2,4},{3,5},{4,6},{5,7},{6,0},{7,1},{8,10},{9,11},{10,... | collective-permute-start | bytes 1769480 | tf_op jit(solution)/shard_map/ppermute | solution.py:573
  206.2 38.6 %collective-permute-start.40 = (bf16[144,2048]{1,0:T(8,128)(2,1)S(1)}, bf16[144,2048]{1,0:T(8,128)(2,1)S(1)}, u32[]{:S(2)}, u32[]{:S(2)}) collective-permute-start(bf16[144,2048]{1,0:T(8,128)(2,1)S(1)} %add_convert_fusion), channel_id=1, source_target_pairs={{0,4},{1,5},{2,6},{3,7},{4,0},{5,1},{6,2},{7,3},{8,12},{9,13},{10,... | collective-permute-start | bytes 1769480 | tf_op jit(solution)/shard_map/ppermute | solution.py:574
  209.8 17.3 %collective-permute-start.43 = (bf16[80,2048]{1,0:T(8,128)(2,1)S(1)}, bf16[80,2048]{1,0:T(8,128)(2,1)S(1)}, u32[]{:S(2)}, u32[]{:S(2)}) collective-permute-start(bf16[80,2048]{1,0:T(8,128)(2,1)S(1)} %copy-done.41), channel_id=1, source_target_pairs={{0,3},{1,2},{2,5},{3,4},{4,7},{5,6},{6,1},{7,0},{8,11},{9,10},{10,... | collective-permute-start | bytes 983048 | tf_op jit(solution)/shard_map/ppermute | solution.py:579
  219.6 26.6 %collective-permute-start.49 = (bf16[64,2048]{1,0:T(8,128)(2,1)S(1)}, bf16[64,2048]{1,0:T(8,128)(2,1)S(1)}, u32[]{:S(2)}, u32[]{:S(2)}) collective-permute-start(bf16[64,2048]{1,0:T(8,128)(2,1)S(1)} %copy-done.47), channel_id=1, source_target_pairs={{0,7},{1,6},{2,1},{3,0},{4,3},{5,2},{6,5},{7,4},{8,15},{9,14},{10,... | collective-permute-start | bytes 786440 | tf_op jit(solution)/shard_map/ppermute | solution.py:582
  227.1 19.2 %collective-permute-start.50 = (bf16[64,2048]{1,0:T(8,128)(2,1)S(1)}, bf16[64,2048]{1,0:T(8,128)(2,1)S(1)}, u32[]{:S(2)}, u32[]{:S(2)}) collective-permute-start(bf16[64,2048]{1,0:T(8,128)(2,1)S(1)} %copy-done.46), channel_id=1, source_target_pairs={{0,3},{1,2},{2,5},{3,4},{4,7},{5,6},{6,1},{7,0},{8,11},{9,10},{10,... | collective-permute-start | bytes 786440 | tf_op jit(solution)/shard_map/ppermute | solution.py:583
  267.4 15.5 %collective-permute-start.48 = (bf16[80,2048]{1,0:T(8,128)(2,1)S(1)}, bf16[80,2048]{1,0:T(8,128)(2,1)S(1)}, u32[]{:S(2)}, u32[]{:S(2)}) collective-permute-start(bf16[80,2048]{1,0:T(8,128)(2,1)S(1)} %collective-permute-done.47.refs_5_), channel_id=1, source_target_pairs={{0,6},{1,7},{2,0},{3,1},{4,2},{5,3},{6,4},{7,5},{8,14},{9,15},{10,... | collective-permute-start | bytes 983048 | tf_op jit(solution)/shard_map/ppermute | solution.py:64
  (82 other events, 1072.3 us)
where the time goes:
time: 288 us
  waiting for transfers between devices  101 us (35%)
  starting transfers between devices  77.3 us (27%)
  Pallas kernels  70.6 us (25%)
  local copies, waits for them, and re-layouts  20.3 us (7%)
  blocking collectives  14.4 us (5%)
  other arithmetic  3.19 us (1%)
    pallas_call x2, Pallas kernels, feed_forward(): pl.pallas_call(functools.partial(feed_forward_kernel, len(pieces), outs),...  23.4 us
    all_to_all x1, blocking collectives, layer(): lax.all_to_all(head_rows, 'tp', split_axis=0, concat_axis=0, tiled=True)  14.4 us
    ppermute x1, waiting for transfers between devices, layer(): lax.ppermute(for_back, 'tp', tp_y(3))  12.2 us
    unnamed x116, local copies, waits for them, and re-layouts  11.9 us
    pallas_call x1, Pallas kernels, first_feed_forward(): pl.pallas_call(functools.partial(first_feed_forward_kernel, len(weights),...  11.9 us
    ppermute x3, waiting for transfers between devices, gather_pair_first(): lax.ppermute(halves(back, axis)[0], name, up)  11.7 us
    pallas_call x1, Pallas kernels, attention(): pl.pallas_call(attention_kernel, out_shape=jax.ShapeDtypeStruct((row_coun...  11.6 us
    ppermute x3, waiting for transfers between devices, gather_pair_first(): own = jnp.concatenate([piece, lax.ppermute(piece, name, flip)], axis=axis)  11.3 us
  transfers between devices with their start and end apart: 61, of which 22 were waited for; matrix products, arithmetic and copies ran while one was open for 5% of the time, Pallas kernels for 23%

commit v1 on v0

--- a/solution.py
+++ b/solution.py
@@ -137,7 +137,7 @@
     rows, width = own_ref.shape[1:]
     first = 0
     for group, count in enumerate(counts):
-        entry = 16 + 8 * group
+        entry = 24 + 8 * group
         term = None
         for weight_ref in weight_refs[:count]:
             for i in range(weight_ref.shape[0] // width):
@@ -507,7 +507,8 @@
     first_two = from_partner(first_one)
     out_block = first_one[:, width:].reshape(half // block, block, heads_width // block, block)
     out_block = out_block.transpose(2, 1, 0, 3).reshape(heads_width, half)
-    out_pieces = gather_pair_first(out_block, 0, TP)
+    ring = gather_ring(out_block, TP)
+    out_pieces = ring + cross_each(ring, TP)
     down_square = down_weight.reshape(ff_local // block, block, block).transpose(1, 0, 2)
     second_pack = jnp.concatenate(
         [gate_up_weight.reshape(block, 2 * ff_local), down_square.reshape(block, ff_local)], axis=1

time: 288 us -> 294 us (1.021)
  blocking collectives: 14.4 us -> 0 us
  starting transfers between devices: 77.3 us -> 88.9 us
  waiting for transfers between devices: 101 us -> 108 us
    ppermute x8 -> x12, waiting for transfers between devices: 10.2 us -> 28.4 us  [cross_each(): return [lax.ppermute(piece, group[0], group[1]) for piece in pieces]]
    all_to_all x1 -> x0, blocking collectives: 14.4 us -> none  [layer(): lax.all_to_all(head_rows, 'tp', split_axis=0, concat_axis=0, tiled=True)]
    ppermute x3 -> x2, waiting for transfers between devices: 11.7 us -> 1.7 us  [gather_pair_first(): lax.ppermute(halves(back, axis)[0], name, up)]
    ppermute x3 -> x2, waiting for transfers between devices: 8.92 us -> 0.01 us  [gather_pair_first(): lax.ppermute(halves(ahead, axis)[1], name, down)]
    all_to_all x0 -> x1, waiting for transfers between devices: none -> 8.83 us  [layer(): lax.all_to_all(head_rows, 'tp', split_axis=0, concat_axis=0, tiled=True)]
    ppermute x8 -> x12, starting transfers between devices: 8 us -> 13.8 us  [cross_each(): return [lax.ppermute(piece, group[0], group[1]) for piece in pieces]]
    ppermute x1 -> x2, waiting for transfers between devices: 2.45 us -> 8.11 us  [gather_ring(): return [piece, back, ahead, lax.ppermute(back, name, up)]]
    ppermute x3 -> x2, starting transfers between devices: 8.67 us -> 3.57 us  [gather_pair_first(): lax.ppermute(halves(ahead, axis)[1], name, down)]
  transfers between devices with their start and end apart: 61 -> 64, of which waited for: 22 -> 24; matrix products, arithmetic and copies ran while one was open for 5% -> 6% of each run, Pallas kernels for 23% -> 23%
where the time goes in v1:
time: 294 us; the launch traced here: 293 us
  waiting for transfers between devices  108 us (37%)
  starting transfers between devices  88.9 us (30%)
  Pallas kernels  70.7 us (24%)
  local copies, waits for them, and re-layouts  22 us (7%)
  other arithmetic  3.16 us (1%)
    ppermute x12, waiting for transfers between devices, cross_each(): return [lax.ppermute(piece, group[0], group[1]) for piece in pieces]  28.4 us
    pallas_call x2, Pallas kernels, feed_forward(): pl.pallas_call(functools.partial(feed_forward_kernel, len(pieces), outs),...  23.4 us
    ppermute x12, starting transfers between devices, cross_each(): return [lax.ppermute(piece, group[0], group[1]) for piece in pieces]  13.8 us
    unnamed x111, local copies, waits for them, and re-layouts  11.9 us
    pallas_call x1, Pallas kernels, first_feed_forward(): pl.pallas_call(functools.partial(first_feed_forward_kernel, len(weights),...  11.8 us
    ppermute x1, waiting for transfers between devices, layer(): lax.ppermute(for_back, 'tp', tp_y(3))  11.8 us
    pallas_call x1, Pallas kernels, attention(): pl.pallas_call(attention_kernel, out_shape=jax.ShapeDtypeStruct((row_coun...  11.6 us
    all_to_all x1, waiting for transfers between devices, layer(): lax.all_to_all(head_rows, 'tp', split_axis=0, concat_axis=0, tiled=True)  8.83 us
  transfers between devices with their start and end apart: 64, of which 24 were waited for; matrix products, arithmetic and copies ran while one was open for 6% of the time, Pallas kernels for 23%

profile of v1, /device:TPU:0, one launch (start us, length us, event | category | flops | bytes accessed | tf_op | source)
XLA Modules:
  0.0 293.1 jit_solution(12204087800207164684)
XLA Ops:
  21.9 3.3 %collective-permute-start.4 = (bf16[128,640]{1,0:T(8,128)(2,1)S(1)}, bf16[128,640]{1,0:T(8,128)(2,1)S(1)}, u32[]{:S(2)}, u32[]{:S(2)}) collective-permute-start(bf16[128,640]{1,0:T(8,128)(2,1)S(1)} %split.17), channel_id=1, source_target_pairs={{0,48},{8,56},{16,0},{24,8},{32,16},{40,24},{48,32},{56,40},{64,11... | collective-permute-start | bytes 491528 | tf_op jit(solution)/shard_map/ppermute | solution.py:47
  29.7 5.0 %collective-permute-done.15 = bf16[128,3072]{1,0:T(8,128)(2,1)S(1)} collective-permute-done((bf16[128,3072]{1,0:T(8,128)(2,1)S(1)}, bf16[128,3072]{1,0:T(8,128)(2,1)S(1)}, u32[]{:S(2)}, u32[]{:S(2)}) %collective-permute-start.15) | collective-permute-done | bytes 786464 | tf_op jit(solution)/shard_map/ppermute | solution.py:42
  34.9 3.2 %collective-permute-start.17 = (bf16[256,3072]{1,0:T(8,128)(2,1)S(1)}, bf16[256,3072]{1,0:T(8,128)(2,1)}, u32[]{:S(2)}, u32[]{:S(2)}) collective-permute-start(bf16[256,3072]{1,0:T(8,128)(2,1)S(1)} %pad_maximum_fusion.refs_0_.refs_10_.refs_20_), channel_id=1, source_target_pairs={{0,48},{8,56},{16,0},{24,8},{32,16},{40,24},{48,32},{56,40},{64,11... | collective-permute-start | bytes 4718600 | tf_op jit(solution)/shard_map/ppermute | solution.py:44
  49.6 7.3 %normed_blocks.1.rows_ref = bf16[1152,2048]{1,0:T(8,128)(2,1)} custom-call(s32[32]{0:T(128)} %compare_select_fusion.3.place_ref, bf16[1152,2048]{1,0:T(8,128)(2,1)} %bitcast.23), custom_call_target="tpu_custom_call" | custom-call | flops 9437184 | bytes 9437184 | tf_op jit(solution)/shard_map/normed_blocks/pallas_call | solution.py:108
  58.3 11.6 %attention.1 = bf16[1152,256]{1,0:T(8,128)(2,1)} custom-call(bf16[1152,2048]{1,0:T(8,128)(2,1)} %normed_blocks.1.rows_ref, bf16[1024,640]{1,0:T(8,128)(2,1)} %constant_dynamic-update-slice_fusion.1.one_ref, bf16[1024,640]{1,0:T(8,128)(2,1)} %collective-permute-done.5.two_ref, f32[384,128]{1,0:T(8,128)} %get-tuple-element.62.cosine_ref, ...), custom_call_target="tpu_custom_call" | custom-call | flops 2264924160 | bytes 6291456 | tf_op jit(solution)/shard_map/attention/pallas_call | solution.py:458
  69.9 4.2 %all-to-all-start = ((bf16[8,144,256]{2,1,0:T(8,128)(2,1)}), bf16[8,144,256]{2,1,0:T(8,128)(2,1)}, u32[]{:S(2)}, u32[]{:S(2)}) async-start(bf16[8,144,256]{2,1,0:T(8,128)(2,1)} %bitcast.28), calls=%async_computation | async-start | bytes 1179648 | tf_op jit(solution)/shard_map/all_to_all | solution.py:527
  77.5 8.8 %all-to-all-done.own_ref = bf16[8,144,256]{2,1,0:T(8,128)(2,1)} async-done(((bf16[8,144,256]{2,1,0:T(8,128)(2,1)}), bf16[8,144,256]{2,1,0:T(8,128)(2,1)}, u32[]{:S(2)}, u32[]{:S(2)}) %all-to-all-start) | async-done | bytes 589856 | tf_op jit(solution)/shard_map/all_to_all | solution.py:527
  86.3 5.8 %collective-permute-done.9.refs_3_ = bf16[256,1024]{1,0:T(8,128)(2,1)} collective-permute-done((bf16[256,1024]{1,0:T(8,128)(2,1)}, bf16[256,1024]{1,0:T(8,128)(2,1)}, u32[]{:S(2)}, u32[]{:S(2)}) %collective-permute-start.9) | collective-permute-done | bytes 524320 | tf_op jit(solution)/shard_map/ppermute | solution.py:72
  96.0 11.2 %collective-permute-done.12.refs_6_ = bf16[256,1024]{1,0:T(8,128)(2,1)S(1)} collective-permute-done((bf16[256,1024]{1,0:T(8,128)(2,1)}, bf16[256,1024]{1,0:T(8,128)(2,1)S(1)}, u32[]{:S(2)}, u32[]{:S(2)}) %collective-permute-start.12) | collective-permute-done | bytes 524320 | tf_op jit(solution)/shard_map/ppermute | solution.py:76
  107.5 8.0 %collective-permute-done.13.refs_7_ = bf16[256,1024]{1,0:T(8,128)(2,1)S(1)} collective-permute-done((bf16[256,1024]{1,0:T(8,128)(2,1)}, bf16[256,1024]{1,0:T(8,128)(2,1)S(1)}, u32[]{:S(2)}, u32[]{:S(2)}) %collective-permute-start.13) | collective-permute-done | bytes 524320 | tf_op jit(solution)/shard_map/ppermute | solution.py:76
  117.1 5.4 %project.1 = (f32[144,1024]{1,0:T(8,128)}, bf16[144,1024]{1,0:T(8,128)(2,1)}) custom-call(s32[32]{0:T(128)} %compare_select_fusion.3.place_ref, bf16[8,144,256]{2,1,0:T(8,128)(2,1)} %all-to-all-done.own_ref, bf16[8,144,256]{2,1,0:T(8,128)(2,1)} %copy-done.7, bf16[256,1024]{1,0:T(8,128)(2,1)} %bitcast.22.refs_0_, ...), custom_call_target="tpu_custom_call" | custom-call | flops 1207959552 | bytes 4194304 | tf_op jit(solution)/shard_map/project/pallas_call | solution.py:162
  125.1 3.5 %combine.1 = (bf16[144,2048]{1,0:T(8,128)(2,1)}, bf16[80,2048]{1,0:T(8,128)(2,1)}, bf16[64,2048]{1,0:T(8,128)(2,1)}, f32[144,128]{1,0:T(8,128)}) custom-call(s32[32]{0:T(128)} %compare_select_fusion.3.place_ref, s32[6]{0:T(128)} %reshape.60.run_ref, s32[1]{0:T(128)} %bitcast.tp_ref, f32[144,1024]{1,0:T(8,128)} %get-tuple-element.32.one_ref, ...), custom_call_target="tpu_custom_call" | custom-call | flops 2359296 | bytes 3538944 | tf_op jit(solution)/shard_map/combine/pallas_call | solution.py:207
  130.2 8.7 %collective-permute-done.25.refs_31_ = bf16[80,2048]{1,0:T(8,128)(2,1)S(1)} collective-permute-done((bf16[80,2048]{1,0:T(8,128)(2,1)}, bf16[80,2048]{1,0:T(8,128)(2,1)S(1)}, u32[]{:S(2)}, u32[]{:S(2)}) %collective-permute-start.25) | collective-permute-done | bytes 327712 | tf_op jit(solution)/shard_map/ppermute | solution.py:535
  144.2 11.8 %first_feed_forward.1 = (bf16[144,2048]{1,0:T(8,128)(2,1)}, bf16[80,2048]{1,0:T(8,128)(2,1)}, bf16[2048,1024]{1,0:T(8,128)(2,1)}, bf16[2048,1024]{1,0:T(8,128)(2,1)}, bf16[1024,2048]{1,0:T(8,128)(2,1)}) custom-call(bf16[256,3072]{1,0:T(8,128)(2,1)} %copy-done, bf16[256,3072]{1,0:T(8,128)(2,1)} %copy-done.1, ...), custom_call_target="tpu_custom_call" | custom-call | flops 2818572288 | bytes 14417920 | tf_op jit(solution)/shard_map/first_feed_forward/pallas_call | solution.py:316
  157.7 3.2 %collective-permute-start.36 = (bf16[80,2048]{1,0:T(8,128)(2,1)S(1)}, bf16[80,2048]{1,0:T(8,128)(2,1)S(1)}, u32[]{:S(2)}, u32[]{:S(2)}) collective-permute-start(bf16[80,2048]{1,0:T(8,128)(2,1)S(1)} %collective-permute-done.29.refs_3_), channel_id=1, source_target_pairs={{0,6},{1,7},{2,0},{3,1},{4,2},{5,3},{6,4},{7,5},{8,14},{9,15},{10,... | collective-permute-start | bytes 983048 | tf_op jit(solution)/shard_map/ppermute | solution.py:547
  161.5 5.0 %collective-permute-done.35.refs_1_ = bf16[64,2048]{1,0:T(8,128)(2,1)S(1)} collective-permute-done((bf16[64,2048]{1,0:T(8,128)(2,1)S(1)}, bf16[64,2048]{1,0:T(8,128)(2,1)S(1)}, u32[]{:S(2)}, u32[]{:S(2)}) %collective-permute-start.35) | collective-permute-done | bytes 262176 | tf_op jit(solution)/shard_map/ppermute | solution.py:548
  170.2 4.0 %collective-permute-start.28 = (bf16[80,2048]{1,0:T(8,128)(2,1)S(1)}, bf16[80,2048]{1,0:T(8,128)(2,1)S(1)}, u32[]{:S(2)}, u32[]{:S(2)}) collective-permute-start(bf16[80,2048]{1,0:T(8,128)(2,1)S(1)} %copy-done.10), channel_id=1, source_target_pairs={{0,6},{1,7},{2,0},{3,1},{4,2},{5,3},{6,4},{7,5},{8,14},{9,15},{10,... | collective-permute-start | bytes 983048 | tf_op jit(solution)/shard_map/ppermute | solution.py:53
  176.5 3.2 %collective-permute-done.37.refs_3_ = bf16[64,2048]{1,0:T(8,128)(2,1)S(1)} collective-permute-done((bf16[64,2048]{1,0:T(8,128)(2,1)S(1)}, bf16[64,2048]{1,0:T(8,128)(2,1)S(1)}, u32[]{:S(2)}, u32[]{:S(2)}) %collective-permute-start.37) | collective-permute-done | bytes 262176 | tf_op jit(solution)/shard_map/ppermute | solution.py:76
  180.4 11.9 %feed_forward.3 = (bf16[144,2048]{1,0:T(8,128)(2,1)}, bf16[144,2048]{1,0:T(8,128)(2,1)}, bf16[64,2048]{1,0:T(8,128)(2,1)}, bf16[64,2048]{1,0:T(8,128)(2,1)}, bf16[64,2048]{1,0:T(8,128)(2,1)}) custom-call(bf16[2048,1024]{1,0:T(8,128)(2,1)} %get-tuple-element.39.gate_ref, bf16[2048,1024]{1,0:T(8,128)(2,1)} %get-tuple-element.40.up_ref, ...), custom_call_target="tpu_custom_call" | custom-call | flops 6039797760 | bytes 16515072 | tf_op jit(solution)/shard_map/feed_forward/pallas_call | solution.py:337
  195.9 11.6 %feed_forward.2 = (bf16[144,2048]{1,0:T(8,128)(2,1)}, bf16[144,2048]{1,0:T(8,128)(2,1)}, bf16[80,2048]{1,0:T(8,128)(2,1)}, bf16[80,2048]{1,0:T(8,128)(2,1)}) custom-call(bf16[2048,1024]{1,0:T(8,128)(2,1)} %get-tuple-element.39.gate_ref, bf16[2048,1024]{1,0:T(8,128)(2,1)} %get-tuple-element.40.up_ref, bf16[1024,2048]{1,0:T(8,128)(2,1)} %get-tuple-element.41.down_ref, ...), custom_call_target="tpu_custom_call" | custom-call | flops 5637144576 | bytes 16252928 | tf_op jit(solution)/shard_map/feed_forward/pallas_call | solution.py:337
  216.0 8.6 %collective-permute-done.44 = bf16[80,2048]{1,0:T(8,128)(2,1)S(1)} collective-permute-done((bf16[80,2048]{1,0:T(8,128)(2,1)}, bf16[80,2048]{1,0:T(8,128)(2,1)S(1)}, u32[]{:S(2)}, u32[]{:S(2)}) %collective-permute-start.44) | collective-permute-done | bytes 327712 | tf_op jit(solution)/shard_map/ppermute | solution.py:579
  224.5 3.4 %collective-permute-start.51 = (bf16[64,2048]{1,0:T(8,128)(2,1)S(1)}, bf16[64,2048]{1,0:T(8,128)(2,1)S(1)}, u32[]{:S(2)}, u32[]{:S(2)}) collective-permute-start(bf16[64,2048]{1,0:T(8,128)(2,1)S(1)} %copy-done.45), channel_id=1, source_target_pairs={{0,7},{1,6},{2,1},{3,0},{4,3},{5,2},{6,5},{7,4},{8,15},{9,14},{10,... | collective-permute-start | bytes 786440 | tf_op jit(solution)/shard_map/ppermute | solution.py:583
  227.9 3.6 %collective-permute-done.45 = bf16[80,2048]{1,0:T(8,128)(2,1)S(1)} collective-permute-done((bf16[80,2048]{1,0:T(8,128)(2,1)S(1)}, bf16[80,2048]{1,0:T(8,128)(2,1)S(1)}, u32[]{:S(2)}, u32[]{:S(2)}) %collective-permute-start.45) | collective-permute-done | bytes 327712 | tf_op jit(solution)/shard_map/ppermute | solution.py:580
  233.7 11.8 %collective-permute-done.32 = bf16[144,2048]{1,0:T(8,128)(2,1)S(1)} collective-permute-done((bf16[144,2048]{1,0:T(8,128)(2,1)}, bf16[144,2048]{1,0:T(8,128)(2,1)S(1)}, u32[]{:S(2)}, u32[]{:S(2)}) %collective-permute-start.32) | collective-permute-done | bytes 589856 | tf_op jit(solution)/shard_map/ppermute | solution.py:573
  250.8 3.9 %collective-permute-done.53 = bf16[64,2048]{1,0:T(8,128)(2,1)S(1)} collective-permute-done((bf16[64,2048]{1,0:T(8,128)(2,1)S(1)}, bf16[64,2048]{1,0:T(8,128)(2,1)S(1)}, u32[]{:S(2)}, u32[]{:S(2)}) %collective-permute-start.53) | collective-permute-done | bytes 262176 | tf_op jit(solution)/shard_map/ppermute | solution.py:585
  255.2 3.4 %collective-permute-start.57 = (bf16[64,2048]{1,0:T(8,128)(2,1)S(1)}, bf16[64,2048]{1,0:T(8,128)(2,1)S(1)}, u32[]{:S(2)}, u32[]{:S(2)}) collective-permute-start(bf16[64,2048]{1,0:T(8,128)(2,1)S(1)} %add_convert_fusion.2.refs_6_), channel_id=1, source_target_pairs={{0,6},{1,7},{2,0},{3,1},{4,2},{5,3},{6,4},{7,5},{8,14},{9,15},{10,... | collective-permute-start | bytes 786440 | tf_op jit(solution)/shard_map/ppermute | solution.py:71
  259.8 3.2 %collective-permute-start.49 = (bf16[80,2048]{1,0:T(8,128)(2,1)S(1)}, bf16[80,2048]{1,0:T(8,128)(2,1)S(1)}, u32[]{:S(2)}, u32[]{:S(2)}) collective-permute-start(bf16[80,2048]{1,0:T(8,128)(2,1)S(1)} %collective-permute-done.48.refs_1_), channel_id=1, source_target_pairs={{0,6},{1,7},{2,0},{3,1},{4,2},{5,3},{6,4},{7,5},{8,14},{9,15},{10,... | collective-permute-start | bytes 983048 | tf_op jit(solution)/shard_map/ppermute | solution.py:62
  263.8 3.8 %collective-permute-start.62 = (bf16[80,2048]{1,0:T(8,128)(2,1)S(1)}, bf16[80,2048]{1,0:T(8,128)(2,1)S(1)}, u32[]{:S(2)}, u32[]{:S(2)}) collective-permute-start(bf16[80,2048]{1,0:T(8,128)(2,1)S(1)} %add_convert_fusion.1.refs_0_), channel_id=1, source_target_pairs={{0,6},{1,7},{2,0},{3,1},{4,2},{5,3},{6,4},{7,5},{8,14},{9,15},{10,... | collective-permute-start | bytes 983048 | tf_op jit(solution)/shard_map/ppermute | solution.py:60
  267.8 3.8 %collective-permute-done.46.refs_2_ = bf16[80,2048]{1,0:T(8,128)(2,1)S(1)} collective-permute-done((bf16[80,2048]{1,0:T(8,128)(2,1)S(1)}, bf16[80,2048]{1,0:T(8,128)(2,1)S(1)}, u32[]{:S(2)}, u32[]{:S(2)}) %collective-permute-start.46) | collective-permute-done | bytes 327712 | tf_op jit(solution)/shard_map/ppermute | solution.py:59
  271.6 3.2 %collective-permute-start.50 = (bf16[80,2048]{1,0:T(8,128)(2,1)S(1)}, bf16[80,2048]{1,0:T(8,128)(2,1)S(1)}, u32[]{:S(2)}, u32[]{:S(2)}) collective-permute-start(bf16[80,2048]{1,0:T(8,128)(2,1)S(1)} %collective-permute-done.49.refs_5_), channel_id=1, source_target_pairs={{0,6},{1,7},{2,0},{3,1},{4,2},{5,3},{6,4},{7,5},{8,14},{9,15},{10,... | collective-permute-start | bytes 983048 | tf_op jit(solution)/shard_map/ppermute | solution.py:64
  281.1 4.2 %place_pieces.2.refs_6_ = bf16[8,144,2048]{2,1,0:T(8,128)(2,1)} custom-call(s32[32]{0:T(128)} %compare_select_fusion.3.place_ref, bf16[80,2048]{1,0:T(8,128)(2,1)} %copy-done.2, bf16[80,2048]{1,0:T(8,128)(2,1)} %copy-done.12, bf16[80,2048]{1,0:T(8,128)(2,1)} %copy-done.14, bf16[80,2048]{1,0:T(8,128)(2,1)} %copy-done.18, bf16[80,2048]{1,0:T(8,128)(2,1)} %copy-done.16, ...), custom_call_target="tpu_custom_call" | custom-call | bytes 6029312 | tf_op jit(solution)/shard_map/place_pieces/pallas_call | solution.py:371
  289.6 3.4 %place_pieces.3 = bf16[8,144,2048]{2,1,0:T(8,128)(2,1)} custom-call(s32[32]{0:T(128)} %compare_select_fusion.3.place_ref, bf16[80,2048]{1,0:T(8,128)(2,1)} %copy-done.15, bf16[80,2048]{1,0:T(8,128)(2,1)} %copy-done.17, bf16[64,2048]{1,0:T(8,128)(2,1)} %copy-done.21, bf16[64,2048]{1,0:T(8,128)(2,1)} %copy-done.25, ...), custom_call_target="tpu_custom_call", output_to_operand_aliasing={{}: (7, {})} | custom-call | bytes 3407872 | tf_op jit(solution)/shard_map/place_pieces/pallas_call | solution.py:371
  (239 shorter events, 99.4 us)
Async XLA Ops:
  15.0 19.7 %collective-permute-start.15 = (bf16[128,3072]{1,0:T(8,128)(2,1)S(1)}, bf16[128,3072]{1,0:T(8,128)(2,1)S(1)}, u32[]{:S(2)}, u32[]{:S(2)}) collective-permute-start(bf16[128,3072]{1,0:T(8,128)(2,1)S(1)} %bitcast_dynamic-update-slice_fusion), channel_id=1, source_target_pairs={{0,64},{8,72},{16,80},{24,88},{32,96},{40,104},{48,112},{56,120},{... | collective-permute-start | bytes 2359304 | tf_op jit(solution)/shard_map/ppermute | solution.py:42
  29.7 27.2 %collective-permute-start.5 = (bf16[1024,640]{1,0:T(8,128)(2,1)}, bf16[1024,640]{1,0:T(8,128)(2,1)}, u32[]{:S(2)}, u32[]{:S(2)}) collective-permute-start(bf16[1024,640]{1,0:T(8,128)(2,1)} %constant_dynamic-update-slice_fusion.1.one_ref), channel_id=1, source_target_pairs={{0,8},{8,0},{16,24},{24,16},{32,40},{40,32},{48,56},{56,48},{64,72... | collective-permute-start | bytes 3932168 | tf_op jit(solution)/shard_map/ppermute | solution.py:497
  34.8 59.4 %collective-permute-start.16 = (bf16[256,3072]{1,0:T(8,128)(2,1)S(1)}, bf16[256,3072]{1,0:T(8,128)(2,1)S(1)}, u32[]{:S(2)}, u32[]{:S(2)}) collective-permute-start(bf16[256,3072]{1,0:T(8,128)(2,1)S(1)} %pad_maximum_fusion.refs_0_.refs_10_.refs_20_), channel_id=1, source_target_pairs={{0,16},{8,24},{16,32},{24,40},{32,48},{40,56},{48,0},{56,8},{64,80... | collective-permute-start | bytes 4718600 | tf_op jit(solution)/shard_map/ppermute | solution.py:43
  34.9 59.4 %collective-permute-start.17 = (bf16[256,3072]{1,0:T(8,128)(2,1)S(1)}, bf16[256,3072]{1,0:T(8,128)(2,1)}, u32[]{:S(2)}, u32[]{:S(2)}) collective-permute-start(bf16[256,3072]{1,0:T(8,128)(2,1)S(1)} %pad_maximum_fusion.refs_0_.refs_10_.refs_20_), channel_id=1, source_target_pairs={{0,48},{8,56},{16,0},{24,8},{32,16},{40,24},{48,32},{56,40},{64,11... | collective-permute-start | bytes 4718600 | tf_op jit(solution)/shard_map/ppermute | solution.py:44
  44.8 29.3 %collective-permute-start.7 = (bf16[256,1024]{1,0:T(8,128)(2,1)}, bf16[256,1024]{1,0:T(8,128)(2,1)}, u32[]{:S(2)}, u32[]{:S(2)}) collective-permute-start(bf16[256,1024]{1,0:T(8,128)(2,1)} %bitcast.22.refs_0_), channel_id=1, source_target_pairs={{0,2},{1,3},{2,4},{3,5},{4,6},{5,7},{6,0},{7,1},{8,10},{9,11},{10,... | collective-permute-start | bytes 1572872 | tf_op jit(solution)/shard_map/ppermute | solution.py:70
  46.4 29.6 %collective-permute-start.8 = (bf16[256,1024]{1,0:T(8,128)(2,1)}, bf16[256,1024]{1,0:T(8,128)(2,1)}, u32[]{:S(2)}, u32[]{:S(2)}) collective-permute-start(bf16[256,1024]{1,0:T(8,128)(2,1)} %bitcast.22.refs_0_), channel_id=1, source_target_pairs={{0,6},{1,7},{2,0},{3,1},{4,2},{5,3},{6,4},{7,5},{8,14},{9,15},{10,... | collective-permute-start | bytes 1572872 | tf_op jit(solution)/shard_map/ppermute | solution.py:71
  56.9 20.6 %collective-permute-start.10 = (bf16[256,1024]{1,0:T(8,128)(2,1)}, bf16[256,1024]{1,0:T(8,128)(2,1)}, u32[]{:S(2)}, u32[]{:S(2)}) collective-permute-start(bf16[256,1024]{1,0:T(8,128)(2,1)} %bitcast.22.refs_0_), channel_id=1, source_target_pairs={{0,1},{1,0},{2,3},{3,2},{4,5},{5,4},{6,7},{7,6},{8,9},{9,8},{10,11... | collective-permute-start | bytes 1572872 | tf_op jit(solution)/shard_map/ppermute | solution.py:76
  74.1 18.1 %collective-permute-start.9 = (bf16[256,1024]{1,0:T(8,128)(2,1)}, bf16[256,1024]{1,0:T(8,128)(2,1)}, u32[]{:S(2)}, u32[]{:S(2)}) collective-permute-start(bf16[256,1024]{1,0:T(8,128)(2,1)} %collective-permute-done.7.refs_1_), channel_id=1, source_target_pairs={{0,2},{1,3},{2,4},{3,5},{4,6},{5,7},{6,0},{7,1},{8,10},{9,11},{10,... | collective-permute-start | bytes 1572872 | tf_op jit(solution)/shard_map/ppermute | solution.py:72
  76.0 17.6 %collective-permute-start.11 = (bf16[256,1024]{1,0:T(8,128)(2,1)}, bf16[256,1024]{1,0:T(8,128)(2,1)}, u32[]{:S(2)}, u32[]{:S(2)}) collective-permute-start(bf16[256,1024]{1,0:T(8,128)(2,1)} %collective-permute-done.7.refs_1_), channel_id=1, source_target_pairs={{0,1},{1,0},{2,3},{3,2},{4,5},{5,4},{6,7},{7,6},{8,9},{9,8},{10,11... | collective-permute-start | bytes 1572872 | tf_op jit(solution)/shard_map/ppermute | solution.py:76
  86.3 29.1 %collective-permute-start.6 = (bf16[8,144,256]{2,1,0:T(8,128)(2,1)}, bf16[8,144,256]{2,1,0:T(8,128)(2,1)S(1)}, u32[]{:S(2)}, u32[]{:S(2)}) collective-permute-start(bf16[8,144,256]{2,1,0:T(8,128)(2,1)} %all-to-all-done.own_ref), channel_id=1, source_target_pairs={{0,8},{8,0},{16,24},{24,16},{32,40},{40,32},{48,56},{56,48},{64,72... | collective-permute-start | bytes 1769480 | tf_op jit(solution)/shard_map/ppermute | solution.py:497
  93.6 21.8 %collective-permute-start.13 = (bf16[256,1024]{1,0:T(8,128)(2,1)}, bf16[256,1024]{1,0:T(8,128)(2,1)S(1)}, u32[]{:S(2)}, u32[]{:S(2)}) collective-permute-start(bf16[256,1024]{1,0:T(8,128)(2,1)} %collective-permute-done.9.refs_3_), channel_id=1, source_target_pairs={{0,1},{1,0},{2,3},{3,2},{4,5},{5,4},{6,7},{7,6},{8,9},{9,8},{10,11... | collective-permute-start | bytes 1572872 | tf_op jit(solution)/shard_map/ppermute | solution.py:76
  94.2 34.5 %collective-permute-start.20 = (bf16[256,3072]{1,0:T(8,128)(2,1)S(1)}, bf16[256,3072]{1,0:T(8,128)(2,1)}, u32[]{:S(2)}, u32[]{:S(2)}) collective-permute-start(bf16[256,3072]{1,0:T(8,128)(2,1)S(1)} %pad_maximum_fusion.refs_0_.refs_10_.refs_20_), channel_id=1, source_target_pairs={{0,8},{8,0},{16,24},{24,16},{32,40},{40,32},{48,56},{56,48},{64,72... | collective-permute-start | bytes 4718600 | tf_op jit(solution)/shard_map/ppermute | solution.py:497
  94.4 28.1 %collective-permute-start.18 = (bf16[128,3072]{1,0:T(8,128)(2,1)S(1)}, bf16[128,3072]{1,0:T(8,128)(2,1)}, u32[]{:S(2)}, u32[]{:S(2)}) collective-permute-start(bf16[128,3072]{1,0:T(8,128)(2,1)S(1)} %split.18), channel_id=1, source_target_pairs={{0,16},{8,24},{16,32},{24,40},{32,48},{40,56},{48,0},{56,8},{64,80... | collective-permute-start | bytes 2359304 | tf_op jit(solution)/shard_map/ppermute | solution.py:46
  115.5 25.5 %collective-permute-start.21 = (bf16[256,3072]{1,0:T(8,128)(2,1)S(1)}, bf16[256,3072]{1,0:T(8,128)(2,1)}, u32[]{:S(2)}, u32[]{:S(2)}) collective-permute-start(bf16[256,3072]{1,0:T(8,128)(2,1)S(1)} %collective-permute-done.16.refs_1_.refs_11_.refs_21_), channel_id=1, source_target_pairs={{0,8},{8,0},{16,24},{24,16},{32,40},{40,32},{48,56},{56,48},{64,72... | collective-permute-start | bytes 4718600 | tf_op jit(solution)/shard_map/ppermute | solution.py:497
  116.2 27.9 %collective-permute-start.22 = (bf16[256,3072]{1,0:T(8,128)(2,1)}, bf16[256,3072]{1,0:T(8,128)(2,1)}, u32[]{:S(2)}, u32[]{:S(2)}) collective-permute-start(bf16[256,3072]{1,0:T(8,128)(2,1)} %collective-permute-done.17.refs_2_.refs_12_.refs_22_), channel_id=1, source_target_pairs={{0,8},{8,0},{16,24},{24,16},{32,40},{40,32},{48,56},{56,48},{64,72... | collective-permute-start | bytes 4718600 | tf_op jit(solution)/shard_map/ppermute | solution.py:497
  122.5 16.9 %collective-permute-start.23 = (bf16[128,3072]{1,0:T(8,128)(2,1)}, bf16[128,3072]{1,0:T(8,128)(2,1)}, u32[]{:S(2)}, u32[]{:S(2)}) collective-permute-start(bf16[128,3072]{1,0:T(8,128)(2,1)} %collective-permute-done.18.refs_3_.refs_13_.refs_23_), channel_id=1, source_target_pairs={{0,8},{8,0},{16,24},{24,16},{32,40},{40,32},{48,56},{56,48},{64,72... | collective-permute-start | bytes 2359304 | tf_op jit(solution)/shard_map/ppermute | solution.py:497
  124.3 16.6 %collective-permute-start.24 = (bf16[128,3072]{1,0:T(8,128)(2,1)}, bf16[128,3072]{1,0:T(8,128)(2,1)}, u32[]{:S(2)}, u32[]{:S(2)}) collective-permute-start(bf16[128,3072]{1,0:T(8,128)(2,1)} %collective-permute-done.19.refs_4_.refs_14_.refs_24_), channel_id=1, source_target_pairs={{0,8},{8,0},{16,24},{24,16},{32,40},{40,32},{48,56},{56,48},{64,72... | collective-permute-start | bytes 2359304 | tf_op jit(solution)/shard_map/ppermute | solution.py:497
  138.9 22.1 %collective-permute-start.31 = (bf16[64,2048]{1,0:T(8,128)(2,1)}, bf16[64,2048]{1,0:T(8,128)(2,1)S(1)}, u32[]{:S(2)}, u32[]{:S(2)}) collective-permute-start(bf16[64,2048]{1,0:T(8,128)(2,1)} %get-tuple-element.37.refs_32_), channel_id=1, source_target_pairs={{0,6},{1,7},{2,0},{3,1},{4,2},{5,3},{6,4},{7,5},{8,14},{9,15},{10,... | collective-permute-start | bytes 786440 | tf_op jit(solution)/shard_map/ppermute | solution.py:53
  139.4 16.6 %collective-permute-start.30 = (bf16[64,2048]{1,0:T(8,128)(2,1)}, bf16[64,2048]{1,0:T(8,128)(2,1)S(1)}, u32[]{:S(2)}, u32[]{:S(2)}) collective-permute-start(bf16[64,2048]{1,0:T(8,128)(2,1)} %get-tuple-element.37.refs_32_), channel_id=1, source_target_pairs={{0,2},{1,3},{2,4},{3,5},{4,6},{5,7},{6,0},{7,1},{8,10},{9,11},{10,... | collective-permute-start | bytes 786440 | tf_op jit(solution)/shard_map/ppermute | solution.py:53
  140.9 16.8 %collective-permute-start.26 = (bf16[80,2048]{1,0:T(8,128)(2,1)}, bf16[80,2048]{1,0:T(8,128)(2,1)S(1)}, u32[]{:S(2)}, u32[]{:S(2)}) collective-permute-start(bf16[80,2048]{1,0:T(8,128)(2,1)} %get-tuple-element.36.refs_30_), channel_id=1, source_target_pairs={{0,2},{1,3},{2,4},{3,5},{4,6},{5,7},{6,0},{7,1},{8,10},{9,11},{10,... | collective-permute-start | bytes 983048 | tf_op jit(solution)/shard_map/ppermute | solution.py:53
  141.0 16.7 %collective-permute-start.29 = (bf16[80,2048]{1,0:T(8,128)(2,1)S(1)}, bf16[80,2048]{1,0:T(8,128)(2,1)S(1)}, u32[]{:S(2)}, u32[]{:S(2)}) collective-permute-start(bf16[80,2048]{1,0:T(8,128)(2,1)S(1)} %collective-permute-done.25.refs_31_), channel_id=1, source_target_pairs={{0,6},{1,7},{2,0},{3,1},{4,2},{5,3},{6,4},{7,5},{8,14},{9,15},{10,... | collective-permute-start | bytes 983048 | tf_op jit(solution)/shard_map/ppermute | solution.py:53
  157.7 18.8 %collective-permute-start.34 = (bf16[80,2048]{1,0:T(8,128)(2,1)S(1)}, bf16[80,2048]{1,0:T(8,128)(2,1)S(1)}, u32[]{:S(2)}, u32[]{:S(2)}) collective-permute-start(bf16[80,2048]{1,0:T(8,128)(2,1)S(1)} %collective-permute-done.26.refs_0_), channel_id=1, source_target_pairs={{0,2},{1,3},{2,4},{3,5},{4,6},{5,7},{6,0},{7,1},{8,10},{9,11},{10,... | collective-permute-start | bytes 983048 | tf_op jit(solution)/shard_map/ppermute | solution.py:546
  157.7 18.7 %collective-permute-start.36 = (bf16[80,2048]{1,0:T(8,128)(2,1)S(1)}, bf16[80,2048]{1,0:T(8,128)(2,1)S(1)}, u32[]{:S(2)}, u32[]{:S(2)}) collective-permute-start(bf16[80,2048]{1,0:T(8,128)(2,1)S(1)} %collective-permute-done.29.refs_3_), channel_id=1, source_target_pairs={{0,6},{1,7},{2,0},{3,1},{4,2},{5,3},{6,4},{7,5},{8,14},{9,15},{10,... | collective-permute-start | bytes 983048 | tf_op jit(solution)/shard_map/ppermute | solution.py:547
  170.2 24.2 %collective-permute-start.28 = (bf16[80,2048]{1,0:T(8,128)(2,1)S(1)}, bf16[80,2048]{1,0:T(8,128)(2,1)S(1)}, u32[]{:S(2)}, u32[]{:S(2)}) collective-permute-start(bf16[80,2048]{1,0:T(8,128)(2,1)S(1)} %copy-done.10), channel_id=1, source_target_pairs={{0,6},{1,7},{2,0},{3,1},{4,2},{5,3},{6,4},{7,5},{8,14},{9,15},{10,... | collective-permute-start | bytes 983048 | tf_op jit(solution)/shard_map/ppermute | solution.py:53
  175.8 18.6 %collective-permute-start.27 = (bf16[80,2048]{1,0:T(8,128)(2,1)}, bf16[80,2048]{1,0:T(8,128)(2,1)S(1)}, u32[]{:S(2)}, u32[]{:S(2)}) collective-permute-start(bf16[80,2048]{1,0:T(8,128)(2,1)} %copy-done.11), channel_id=1, source_target_pairs={{0,2},{1,3},{2,4},{3,5},{4,6},{5,7},{6,0},{7,1},{8,10},{9,11},{10,... | collective-permute-start | bytes 983048 | tf_op jit(solution)/shard_map/ppermute | solution.py:53
  192.3 18.1 %collective-permute-start.41 = (bf16[144,2048]{1,0:T(8,128)(2,1)}, bf16[144,2048]{1,0:T(8,128)(2,1)S(1)}, u32[]{:S(2)}, u32[]{:S(2)}) collective-permute-start(bf16[144,2048]{1,0:T(8,128)(2,1)} %get-tuple-element.51), channel_id=1, source_target_pairs={{0,1},{1,0},{2,3},{3,2},{4,5},{5,4},{6,7},{7,6},{8,9},{9,8},{10,11... | collective-permute-start | bytes 1769480 | tf_op jit(solution)/shard_map/ppermute | solution.py:569
  193.8 21.0 %collective-permute-start.43 = (bf16[80,2048]{1,0:T(8,128)(2,1)S(1)}, bf16[80,2048]{1,0:T(8,128)(2,1)S(1)}, u32[]{:S(2)}, u32[]{:S(2)}) collective-permute-start(bf16[80,2048]{1,0:T(8,128)(2,1)S(1)} %copy-done.33), channel_id=1, source_target_pairs={{0,1},{1,0},{2,3},{3,2},{4,5},{5,4},{6,7},{7,6},{8,9},{9,8},{10,11... | collective-permute-start | bytes 983048 | tf_op jit(solution)/shard_map/ppermute | solution.py:578
  207.5 38.0 %collective-permute-start.32 = (bf16[144,2048]{1,0:T(8,128)(2,1)}, bf16[144,2048]{1,0:T(8,128)(2,1)S(1)}, u32[]{:S(2)}, u32[]{:S(2)}) collective-permute-start(bf16[144,2048]{1,0:T(8,128)(2,1)} %get-tuple-element.42), channel_id=1, source_target_pairs={{0,6},{1,7},{2,0},{3,1},{4,2},{5,3},{6,4},{7,5},{8,14},{9,15},{10,... | collective-permute-start | bytes 1769480 | tf_op jit(solution)/shard_map/ppermute | solution.py:573
  210.4 38.4 %collective-permute-start.33 = (bf16[144,2048]{1,0:T(8,128)(2,1)}, bf16[144,2048]{1,0:T(8,128)(2,1)S(1)}, u32[]{:S(2)}, u32[]{:S(2)}) collective-permute-start(bf16[144,2048]{1,0:T(8,128)(2,1)} %get-tuple-element.43), channel_id=1, source_target_pairs={{0,2},{1,3},{2,4},{3,5},{4,6},{5,7},{6,0},{7,1},{8,10},{9,11},{10,... | collective-permute-start | bytes 1769480 | tf_op jit(solution)/shard_map/ppermute | solution.py:574
  210.6 38.2 %collective-permute-start.42 = (bf16[144,2048]{1,0:T(8,128)(2,1)S(1)}, bf16[144,2048]{1,0:T(8,128)(2,1)S(1)}, u32[]{:S(2)}, u32[]{:S(2)}) collective-permute-start(bf16[144,2048]{1,0:T(8,128)(2,1)S(1)} %add_convert_fusion), channel_id=1, source_target_pairs={{0,4},{1,5},{2,6},{3,7},{4,0},{5,1},{6,2},{7,3},{8,12},{9,13},{10,... | collective-permute-start | bytes 1769480 | tf_op jit(solution)/shard_map/ppermute | solution.py:575
  224.5 26.3 %collective-permute-start.51 = (bf16[64,2048]{1,0:T(8,128)(2,1)S(1)}, bf16[64,2048]{1,0:T(8,128)(2,1)S(1)}, u32[]{:S(2)}, u32[]{:S(2)}) collective-permute-start(bf16[64,2048]{1,0:T(8,128)(2,1)S(1)} %copy-done.45), channel_id=1, source_target_pairs={{0,7},{1,6},{2,1},{3,0},{4,3},{5,2},{6,5},{7,4},{8,15},{9,14},{10,... | collective-permute-start | bytes 786440 | tf_op jit(solution)/shard_map/ppermute | solution.py:583
  231.5 19.3 %collective-permute-start.52 = (bf16[64,2048]{1,0:T(8,128)(2,1)S(1)}, bf16[64,2048]{1,0:T(8,128)(2,1)S(1)}, u32[]{:S(2)}, u32[]{:S(2)}) collective-permute-start(bf16[64,2048]{1,0:T(8,128)(2,1)S(1)} %copy-done.44), channel_id=1, source_target_pairs={{0,3},{1,2},{2,5},{3,4},{4,7},{5,6},{6,1},{7,0},{8,11},{9,10},{10,... | collective-permute-start | bytes 786440 | tf_op jit(solution)/shard_map/ppermute | solution.py:584
  (83 other events, 1126.2 us)
